TPU v7x, 512 devices: a whole 4x4x16 slice. The times are simulated.
512 devices in a mesh: row: 16 (over y_hi, x, core), col: 32 (over y_lo, z).
Axes of the slice: x: 4, y: 4 (y_hi: 2, y_lo: 2; y = y_hi * 2 + y_lo), z: 16, core: 2. Of those that a mesh axis runs over, the one named last changes fastest.
Arguments:
- inputs: bfloat16 [256, 512, 256], P('row', 'col'), may hold values from -6 to 6
- stored: bfloat16 [256, 512, 256], P('row', 'col'), may hold values from -6 to 6
- upstream: bfloat16 [256, 512, 256], P('row', 'col'), may hold values from -6 to 6
- weight_in: bfloat16 [256, 1024], replicated, may hold values from -0.375 to 0.375
- weight_out: bfloat16 [1024, 256], replicated, may hold values from -0.1875 to 0.1875
- kernel: bfloat16 [27, 27, 256], replicated, may hold values from -0.21875 to 0.21875
Outputs:
- grad_inputs: bfloat16 [256, 512, 256], P('row', 'col')
- grad_weight_in: bfloat16 [256, 1024], replicated
- grad_weight_out: bfloat16 [1024, 256], replicated
- grad_kernel: bfloat16 [27, 27, 256], replicated
All inputs are finite; a program needn't handle non-finite values.
Results may differ from a plain program's by a relative error of at most 0.0052.
Values may be sent and summed in bfloat16 or wider, within the bound.
No kernel may reach another device: no remote copies, remote signals or barrier semaphores. Data moves between devices by JAX's collectives and lax.ppermute only.
A program may use at most 64 MiB of HBM per device.

v0:
```python
import math

import jax
import jax.numpy as jnp
from jax import lax
from jax.sharding import PartitionSpec as P

KS = 27


gelu_coef = 0.044715
root_coef = math.sqrt(2.0 / math.pi)


def padded_2(block, sides, width):
    for axis, dim in sides:
        count = lax.axis_size(axis)
        forward = [(i, i + 1) for i in range(count - 1)]
        backward = [(target, source) for source, target in forward]
        low = lax.ppermute(
            lax.slice_in_dim(block, block.shape[dim] - width, None, axis=dim), axis, forward
        )
        high = lax.ppermute(lax.slice_in_dim(block, 0, width, axis=dim), axis, backward)
        block = jnp.concatenate([low, block, high], axis=dim)
    return block


def gelu_parts(values):
    tanh_part = jnp.tanh(root_coef * (values + gelu_coef * values * values * values))
    result = 0.5 * values * (1.0 + tanh_part)
    slopes = 0.5 * (1.0 + tanh_part) + 0.5 * values * (1.0 - tanh_part * tanh_part) * root_coef * (
        1.0 + 3.0 * gelu_coef * values * values
    )
    return (result, slopes)


def per_device(inputs, stored, upstream, weight_in, weight_out, kernel):
    tile_rows, tile_cols, channels = stored.shape
    radius = KS // 2
    padded_in = padded_2(inputs, (("row", 0), ("col", 1)), radius)
    flat_z = stored.reshape(tile_rows * tile_cols, channels)
    flat_g = upstream.reshape(tile_rows * tile_cols, channels)
    hidden = jnp.dot(flat_z, weight_in, preferred_element_type=jnp.float32)
    values, slopes = gelu_parts(hidden)
    active = values.astype(jnp.bfloat16)
    back_proj = jnp.einsum("nc,fc->nf", flat_g, weight_out, preferred_element_type=jnp.float32)
    grad_hidden = (back_proj * slopes).astype(jnp.bfloat16)
    grad_flat = (
        flat_g.astype(jnp.float32)
        + jnp.einsum("nf,cf->nc", grad_hidden, weight_in, preferred_element_type=jnp.float32)
    ).astype(jnp.bfloat16)
    sum_in = jnp.einsum("nc,nf->cf", flat_z, grad_hidden, preferred_element_type=jnp.float32)
    sum_out = jnp.einsum("nf,nc->fc", active, flat_g, preferred_element_type=jnp.float32)
    grad_mid = grad_flat.reshape(tile_rows, tile_cols, channels)
    padded = padded_2(grad_mid, (("row", 0), ("col", 1)), radius)
    kernel_wide = kernel.astype(jnp.float32)

    def sweep(row_off, state_pair):
        accumulated, kernel_sums = state_pair
        slab_rows = lax.dynamic_slice_in_dim(padded, 2 * radius - row_off, tile_rows, 0)
        tap_row = lax.dynamic_index_in_dim(kernel_wide, row_off, 0, keepdims=False)
        tap_sums = []
        source_rows = lax.dynamic_slice_in_dim(padded_in, row_off, tile_rows, 0)
        for offset in range(KS):
            shifted = slab_rows[:, 2 * radius - offset : 2 * radius - offset + tile_cols].astype(
                jnp.float32
            )
            accumulated = accumulated + tap_row[offset] * shifted
            tap_sums.append(
                jnp.sum(
                    source_rows[:, offset : offset + tile_cols].astype(jnp.float32)
                    * grad_mid.astype(jnp.float32),
                    axis=(0, 1),
                )
            )
        kernel_sums = lax.dynamic_update_index_in_dim(kernel_sums, jnp.stack(tap_sums), row_off, 0)
        return (accumulated, kernel_sums)

    start = (
        jnp.zeros((tile_rows, tile_cols, channels), jnp.float32),
        jnp.zeros((KS, KS, channels), jnp.float32),
    )
    accumulated, kernel_sums = lax.fori_loop(0, KS, sweep, start)
    grad_inputs = (grad_mid.astype(jnp.float32) + accumulated).astype(jnp.bfloat16)
    devices_all = lax.axis_size("row") * lax.axis_size("col")
    pixel_count = tile_rows * tile_cols * devices_all
    grad_scale = 1.0 / math.sqrt(pixel_count)
    total_in, total_out, total_kernel = lax.psum((sum_in, sum_out, kernel_sums), ("row", "col"))
    final_in = (total_in * grad_scale).astype(jnp.bfloat16)
    final_out = (total_out * grad_scale).astype(jnp.bfloat16)
    final_kernel = (total_kernel * grad_scale).astype(jnp.bfloat16)
    return (grad_inputs, final_in, final_out, final_kernel)


def solution(mesh):
    return jax.shard_map(
        per_device,
        mesh=mesh,
        in_specs=(
            P("row", "col", None),
            P("row", "col", None),
            P("row", "col", None),
            P(),
            P(),
            P(),
        ),
        out_specs=(P("row", "col", None), P(), P(), P()),
        check_vma=False,
    )
```

profile of v0, /device:TPU:1, one launch (start us, length us, event | category | flops | bytes accessed | tf_op | source)
XLA Modules:
  0.0 735.3 jit_solution(15265155077819901932)
XLA Ops:
  8.3 8.7 %collective-permute-start.5 = (bf16[13,16,256]{2,1,0:T(8,128)(2,1)S(1)}, bf16[13,16,256]{2,1,0:T(8,128)(2,1)S(1)}, u32[]{:S(2)}, u32[]{:S(2)}) collective-permute-start(bf16[13,16,256]{2,1,0:T(8,128)(2,1)S(1)} %get-tuple-element.286), channel_id=1, source_target_pairs={{32,0},{64,32},{96,64},{128,96},{160,128},{192,160},{224,192},{256... | collective-permute-start | bytes 319496 | tf_op jit(solution)/shard_map/ppermute | solution.py:23
  17.1 1.9 collective-permute-start.4
  21.4 2.4 collective-permute-start.1
  23.8 3.3 collective-permute-start
  27.1 1.6 fusion.58
  30.0 1.4 collective-permute-start.6
  31.4 1.3 collective-permute-start.7
  32.9 4.0 collective-permute-start.2
  36.9 1.3 collective-permute-start.3
  38.2 1.4 convolution_bitcast_fusion
  39.6 3.7 collective-permute-done.7
  43.8 2.2 collective-permute-done.2
  46.0 4.1 collective-permute-done.3
  50.6 179.6 %while.18 = (s32[]{:T(128)}, f32[16,16,256]{2,1,0:T(8,128)S(1)}, f32[27,27,256]{2,1,0:T(8,128)}, f32[27,27,256]{2,1,0:T(8,128)}, bf16[42,42,256]{2,1,0:T(8,128)(...) while((s32[]{:T(128)}, f32[16,16,256]{2,1,0:T(8,128)S(1)}, ...), condition=%wide.region_28.29_spmd.clone, body=%wide.region_0.28_spmd.clone.sunk | while | flops 10806561 | bytes 8091653 | solution.py:83
  52.2 1.2 fusion.83
  54.6 2.1 multiply_add_fusion.3
  58.8 1.2 fusion.83
  61.2 2.1 multiply_add_fusion.3
  65.4 1.2 fusion.83
  67.9 2.1 multiply_add_fusion.3
  72.1 1.2 fusion.83
  73.4 1.2 constant_dynamic-slice_fusion.30
  74.7 2.1 multiply_add_fusion.3
  78.9 1.2 fusion.83
  81.3 2.1 multiply_add_fusion.3
  85.5 1.2 fusion.83
  87.9 2.1 multiply_add_fusion.3
  92.2 1.2 fusion.83
  94.6 2.1 multiply_add_fusion.3
  98.8 1.2 fusion.83
  101.2 2.1 multiply_add_fusion.3
  105.4 1.2 fusion.83
  107.9 2.1 multiply_add_fusion.3
  112.1 1.2 fusion.83
  114.5 2.1 multiply_add_fusion.3
  118.7 1.2 fusion.83
  121.1 2.1 multiply_add_fusion.3
  125.3 1.2 fusion.83
  127.8 2.1 multiply_add_fusion.3
  132.0 1.2 fusion.83
  134.4 2.1 multiply_add_fusion.3
  138.6 1.2 fusion.83
  141.1 2.1 multiply_add_fusion.3
  147.7 2.1 multiply_add_fusion.3
  151.9 1.2 fusion.83
  154.4 2.1 multiply_add_fusion.3
  161.0 2.1 multiply_add_fusion.3
  165.2 1.2 fusion.83
  167.7 2.1 multiply_add_fusion.3
  174.3 2.1 multiply_add_fusion.3
  178.5 1.2 fusion.83
  180.9 2.1 multiply_add_fusion.3
  187.6 2.1 multiply_add_fusion.3
  191.8 1.2 fusion.83
  194.2 2.1 multiply_add_fusion.3
  200.9 2.1 multiply_add_fusion.3
  205.1 1.2 fusion.83
  207.5 2.1 multiply_add_fusion.3
  214.2 2.1 multiply_add_fusion.3
  218.4 1.2 fusion.83
  220.8 2.1 multiply_add_fusion.3
  227.4 2.1 multiply_add_fusion.3
  230.9 493.4 %all-reduce.3.cloned.1.call-done = (f32[256,1024]{0,1:T(8,128)}, f32[1024,256]{1,0:T(8,128)}, f32[27,27,256]{2,1,0:T(8,128)}) async-done(((f32[256,1024]{0,1:T(8,128)}, f32[1024,256]{1,0:T(8,128)}, f32[27,27,256]{2,1,0:T(8,128)}), (f32[256,1024]{0,1:T(8,128)}, f32[1024,256]{1,0:T(8,128)}, f32[27,27,256]{2,1,0:T(8,128)})) %all-reduce.3.cloned.1.call-update) | async-done | bytes 2843664 | tf_op jit(solution)/shard_map/psum | solution.py:88
  724.3 1.4 multiply_convert_fusion.2
  (184 shorter events, 106.0 us)
Async XLA Ops:
  7.2 11.8 %copy-start = (bf16[256,1024]{1,0:T(8,128)(2,1)S(1)}, bf16[256,1024]{1,0:T(8,128)(2,1)}, u32[]{:S(2)}) copy-start(bf16[256,1024]{1,0:T(8,128)(2,1)} %param.11) | copy-start | bytes 1572868
  7.2 13.0 %copy-start.7 = (bf16[1024,256]{1,0:T(8,128)(2,1)S(1)}, bf16[1024,256]{1,0:T(8,128)(2,1)}, u32[]{:S(2)}) copy-start(bf16[1024,256]{1,0:T(8,128)(2,1)} %param.12) | copy-start | bytes 1572868
  7.2 13.0 %copy-start.6 = (bf16[16,16,256]{2,1,0:T(8,128)(2,1)S(1)}, bf16[16,16,256]{2,1,0:T(8,128)(2,1)}, u32[]{:S(2)}) copy-start(bf16[16,16,256]{2,1,0:T(8,128)(2,1)} %param.10) | copy-start | bytes 393220
  7.2 717.1 %all-reduce.3.cloned.1.call-start = ((), (), s32[]{:S(2)}) async-start(), calls=%async_computation | async-start | bytes 5963776 | tf_op jit(solution)/shard_map/psum | solution.py:88
  8.3 21.5 %collective-permute-start.5 = (bf16[13,16,256]{2,1,0:T(8,128)(2,1)S(1)}, bf16[13,16,256]{2,1,0:T(8,128)(2,1)S(1)}, u32[]{:S(2)}, u32[]{:S(2)}) collective-permute-start(bf16[13,16,256]{2,1,0:T(8,128)(2,1)S(1)} %get-tuple-element.286), channel_id=1, source_target_pairs={{32,0},{64,32},{96,64},{128,96},{160,128},{192,160},{224,192},{256... | collective-permute-start | bytes 319496 | tf_op jit(solution)/shard_map/ppermute | solution.py:23
  17.1 12.7 %collective-permute-start.4 = (bf16[13,16,256]{2,1,0:T(8,128)(2,1)S(1)}, bf16[13,16,256]{2,1,0:T(8,128)(2,1)S(1)}, u32[]{:S(2)}, u32[]{:S(2)}) collective-permute-start(bf16[13,16,256]{2,1,0:T(8,128)(2,1)S(1)} %get-tuple-element.287), channel_id=1, source_target_pairs={{0,32},{32,64},{64,96},{96,128},{128,160},{160,192},{192,224},{224... | collective-permute-start | bytes 319496 | tf_op jit(solution)/shard_map/ppermute | solution.py:20
  21.4 11.3 %collective-permute-start.1 = (bf16[13,16,256]{2,1,0:T(8,128)(2,1)S(1)}, bf16[13,16,256]{2,1,0:T(8,128)(2,1)S(1)}, u32[]{:S(2)}, u32[]{:S(2)}) collective-permute-start(bf16[13,16,256]{2,1,0:T(8,128)(2,1)S(1)} %bitcast.191), channel_id=1, source_target_pairs={{32,0},{64,32},{96,64},{128,96},{160,128},{192,160},{224,192},{256... | collective-permute-start | bytes 319496 | tf_op jit(solution)/shard_map/ppermute | solution.py:23
  23.8 4.9 copy-start.5
  23.8 8.9 %collective-permute-start = (bf16[13,16,256]{2,1,0:T(8,128)(2,1)S(1)}, bf16[13,16,256]{2,1,0:T(8,128)(2,1)S(1)}, u32[]{:S(2)}, u32[]{:S(2)}) collective-permute-start(bf16[13,16,256]{2,1,0:T(8,128)(2,1)S(1)} %bitcast.190), channel_id=1, source_target_pairs={{0,32},{32,64},{64,96},{96,128},{128,160},{160,192},{192,224},{224... | collective-permute-start | bytes 319496 | tf_op jit(solution)/shard_map/ppermute | solution.py:20
  28.7 1.0 copy-start.2
  29.9 8.3 %copy-start.4 = (bf16[16,16,256]{2,1,0:T(8,128)(2,1)S(1)}, bf16[16,16,256]{2,1,0:T(8,128)(2,1)}, u32[]{:S(2)}) copy-start(bf16[16,16,256]{2,1,0:T(8,128)(2,1)} %param.9) | copy-start | bytes 393220
  30.0 9.7 %collective-permute-start.6 = (bf16[42,13,256]{2,1,0:T(8,128)(2,1)S(1)}, bf16[42,13,256]{2,1,0:T(8,128)(2,1)S(1)}, u32[]{:S(2)}, u32[]{:S(2)}) collective-permute-start(bf16[42,13,256]{2,1,0:T(8,128)(2,1)S(1)} %get-tuple-element.282), channel_id=1, source_target_pairs={{0,1},{1,2},{2,3},{3,4},{4,5},{5,6},{6,7},{7,8},{8,9},{9,10},{10,1... | collective-permute-start | bytes 838664 | tf_op jit(solution)/shard_map/ppermute | solution.py:20
  31.4 12.0 %collective-permute-start.7 = (bf16[42,13,256]{2,1,0:T(8,128)(2,1)S(1)}, bf16[42,13,256]{2,1,0:T(8,128)(2,1)S(1)}, u32[]{:S(2)}, u32[]{:S(2)}) collective-permute-start(bf16[42,13,256]{2,1,0:T(8,128)(2,1)S(1)} %get-tuple-element.283), channel_id=1, source_target_pairs={{1,0},{2,1},{3,2},{4,3},{5,4},{6,5},{7,6},{8,7},{9,8},{10,9},{11,1... | collective-permute-start | bytes 838664 | tf_op jit(solution)/shard_map/ppermute | solution.py:23
  32.9 13.1 %collective-permute-start.2 = (bf16[42,13,256]{2,1,0:T(8,128)(2,1)S(1)}, bf16[42,13,256]{2,1,0:T(8,128)(2,1)S(1)}, u32[]{:S(2)}, u32[]{:S(2)}) collective-permute-start(bf16[42,13,256]{2,1,0:T(8,128)(2,1)S(1)} %get-tuple-element.284), channel_id=1, source_target_pairs={{0,1},{1,2},{2,3},{3,4},{4,5},{5,6},{6,7},{7,8},{8,9},{9,10},{10,1... | collective-permute-start | bytes 838664 | tf_op jit(solution)/shard_map/ppermute | solution.py:20
  36.9 13.2 %collective-permute-start.3 = (bf16[42,13,256]{2,1,0:T(8,128)(2,1)S(1)}, bf16[42,13,256]{2,1,0:T(8,128)(2,1)S(1)}, u32[]{:S(2)}, u32[]{:S(2)}) collective-permute-start(bf16[42,13,256]{2,1,0:T(8,128)(2,1)S(1)} %get-tuple-element.285), channel_id=1, source_target_pairs={{1,0},{2,1},{3,2},{4,3},{5,4},{6,5},{7,6},{8,7},{9,8},{10,9},{11,1... | collective-permute-start | bytes 838664 | tf_op jit(solution)/shard_map/ppermute | solution.py:23
  724.3 2.4 copy-start.3
  725.7 1.9 copy-start.1
Sparse Core Ops, SparseCore 0:
  230.3 493.9 all-reduce.2
where the time goes:
time: 740 us; the launch traced here: 735 us
  waiting for transfers between devices  504 us (68%)
  other arithmetic  110 us (15%)
  local copies, waits for them, and re-layouts  77.1 us (10%)
  starting transfers between devices  24.4 us (3%)
  between operations  14.3 us (2%)
    psum x1, waiting for transfers between devices, per_device(): lax.psum((sum_in, sum_out, kernel_sums), ('row', 'col'))  493 us
    add x27, other arithmetic, sweep(): accumulated = accumulated + tap_row[offset] * shifted  56.6 us
    slice x54, local copies, waits for them, and re-layouts, sweep(): accumulated = accumulated + tap_row[offset] * shifted  55.3 us
    reduce_sum x54, other arithmetic, sweep(): jnp.sum(source_rows[:, offset:offset + tile_cols].astype(jnp.float32) * g...  47.9 us
    dynamic_update_slice x27, local copies, waits for them, and re-layouts, sweep(): lax.dynamic_update_index_in_dim(kernel_sums, jnp.stack(tap_sums), row_off...  16.5 us
  transfers between devices with their start and end apart: 9, of which 4 were waited for; matrix products, arithmetic and copies ran while one was open for 1% of the time, Pallas kernels for 0%

commit v1 on v0

--- a/solution.py
+++ b/solution.py
@@ -3,9 +3,13 @@
 import jax
 import jax.numpy as jnp
 from jax import lax
-from jax.sharding import PartitionSpec as P
+from jax.sharding import Mesh, PartitionSpec as P
 
 KS = 27
+ROW = ("yh", "x", "core")
+COL = ("yl", "z")
+PLANE = ("x", "yh", "yl")
+LANES = 128
 
 
 gelu_coef = 0.044715
@@ -34,10 +38,41 @@
     return (result, slopes)
 
 
+def to_rows(block):
+    rows, cols = block.shape
+    return block.reshape(rows // 8, 8, cols // LANES, LANES).transpose(0, 2, 1, 3).reshape(-1, LANES)
+
+
+def from_rows(flat, shape):
+    rows, cols = shape
+    return flat.reshape(rows // 8, cols // LANES, 8, LANES).transpose(0, 2, 1, 3).reshape(rows, cols)
+
+
+def scatter_sum(block, axes):
+    count = lax.axis_size(axes)
+    parts = block.reshape(count, block.shape[0] // count, LANES)
+    arrived = lax.all_to_all(parts, axes, 0, 0)
+    return jnp.sum(arrived.astype(jnp.float32), axis=0)
+
+
+def gathered(block, axes):
+    count = lax.axis_size(axes)
+    copies = jnp.broadcast_to(block[None], (count,) + block.shape)
+    return lax.all_to_all(copies, axes, 0, 0).reshape(count * block.shape[0], LANES)
+
+
+def summed(blocks, scale):
+    flat = jnp.concatenate([to_rows(block.astype(jnp.bfloat16)) for block in blocks], axis=0)
+    half = scatter_sum(flat, "core")
+    part = scatter_sum(half.astype(jnp.bfloat16), PLANE)
+    total = (scatter_sum(part, "z") * scale).astype(jnp.bfloat16)
+    return gathered(gathered(gathered(total, "z"), PLANE), "core")
+
+
 def per_device(inputs, stored, upstream, weight_in, weight_out, kernel):
     tile_rows, tile_cols, channels = stored.shape
     radius = KS // 2
-    padded_in = padded_2(inputs, (("row", 0), ("col", 1)), radius)
+    padded_in = padded_2(inputs, ((ROW, 0), (COL, 1)), radius)
     flat_z = stored.reshape(tile_rows * tile_cols, channels)
     flat_g = upstream.reshape(tile_rows * tile_cols, channels)
     hidden = jnp.dot(flat_z, weight_in, preferred_element_type=jnp.float32)
@@ -52,7 +87,7 @@
     sum_in = jnp.einsum("nc,nf->cf", flat_z, grad_hidden, preferred_element_type=jnp.float32)
     sum_out = jnp.einsum("nf,nc->fc", active, flat_g, preferred_element_type=jnp.float32)
     grad_mid = grad_flat.reshape(tile_rows, tile_cols, channels)
-    padded = padded_2(grad_mid, (("row", 0), ("col", 1)), radius)
+    padded = padded_2(grad_mid, ((ROW, 0), (COL, 1)), radius)
     kernel_wide = kernel.astype(jnp.float32)
 
     def sweep(row_off, state_pair):
@@ -82,28 +117,23 @@
     )
     accumulated, kernel_sums = lax.fori_loop(0, KS, sweep, start)
     grad_inputs = (grad_mid.astype(jnp.float32) + accumulated).astype(jnp.bfloat16)
-    devices_all = lax.axis_size("row") * lax.axis_size("col")
-    pixel_count = tile_rows * tile_cols * devices_all
+    pixel_count = tile_rows * tile_cols * lax.axis_size(ROW) * lax.axis_size(COL)
     grad_scale = 1.0 / math.sqrt(pixel_count)
-    total_in, total_out, total_kernel = lax.psum((sum_in, sum_out, kernel_sums), ("row", "col"))
-    final_in = (total_in * grad_scale).astype(jnp.bfloat16)
-    final_out = (total_out * grad_scale).astype(jnp.bfloat16)
-    final_kernel = (total_kernel * grad_scale).astype(jnp.bfloat16)
+    taps = jnp.pad(kernel_sums.reshape(KS * KS, channels), ((0, 768 - KS * KS), (0, 0)))
+    final = summed([sum_in, sum_out, taps], grad_scale)
+    rows_in = sum_in.size // LANES
+    final_in = from_rows(final[:rows_in], sum_in.shape)
+    final_out = from_rows(final[rows_in : 2 * rows_in], sum_out.shape)
+    final_kernel = from_rows(final[2 * rows_in :], taps.shape)[: KS * KS].reshape(KS, KS, channels)
     return (grad_inputs, final_in, final_out, final_kernel)
 
 
 def solution(mesh):
+    fine = Mesh(mesh.devices.reshape(2, 4, 2, 2, 16), ("yh", "x", "core", "yl", "z"))
     return jax.shard_map(
         per_device,
-        mesh=mesh,
-        in_specs=(
-            P("row", "col", None),
-            P("row", "col", None),
-            P("row", "col", None),
-            P(),
-            P(),
-            P(),
-        ),
-        out_specs=(P("row", "col", None), P(), P(), P()),
+        mesh=fine,
+        in_specs=(P(ROW, COL, None), P(ROW, COL, None), P(ROW, COL, None), P(), P(), P()),
+        out_specs=(P(ROW, COL, None), P(), P(), P()),
         check_vma=False,
     )

time: 740 us -> 466 us (0.63)
  waiting for transfers between devices: 504 us -> 19.7 us
  local copies, waits for them, and re-layouts: 77.1 us -> 175 us
  blocking collectives: 0 us -> 75.7 us
  other arithmetic: 110 us -> 156 us
  between operations: 14.3 us -> 1.01 us
    psum x1 -> x0, waiting for transfers between devices: 493 us -> none  [per_device(): lax.psum((sum_in, sum_out, kernel_sums), ('row', 'col'))]
    all_to_all x0 -> x5, blocking collectives: none -> 75.7 us  [the longest x3 49.8 us: scatter_sum(): arrived = lax.all_to_all(parts, axes, 0, 0)]
    another operation x27, local copies, waits for them, and re-layouts: 2.9 us -> 77.1 us  [sweep(): jnp.stack(tap_sums)]
    reduce_sum x54, other arithmetic: 47.9 us -> 79 us  [sweep(): jnp.sum(source_rows[:, offset:offset + tile_cols].astype(jnp.float32) * g...]
    add x27, other arithmetic: 56.6 us -> 73.8 us  [sweep(): accumulated = accumulated + tap_row[offset] * shifted]
    slice x54, local copies, waits for them, and re-layouts: 55.3 us -> 71.8 us  [sweep(): accumulated = accumulated + tap_row[offset] * shifted]
    all_to_all x0 -> x1, waiting for transfers between devices: none -> 9.43 us  [gathered(): lax.all_to_all(copies, axes, 0, 0).reshape(count * block.shape[0], LANES)]
  transfers between devices with their start and end apart: 9 -> 9, of which waited for: 4 -> 4; matrix products, arithmetic and copies ran while one was open for 1% -> 2% of each run, Pallas kernels for 0% -> 0%
where the time goes in v1:
time: 466 us; the launch traced here: 460 us
  local copies, waits for them, and re-layouts  175 us (38%)
  other arithmetic  156 us (33%)
  blocking collectives  75.7 us (16%)
  starting transfers between devices  27.8 us (6%)
  waiting for transfers between devices  19.7 us (4%)
    reduce_sum x54, other arithmetic, sweep(): jnp.sum(source_rows[:, offset:offset + tile_cols].astype(jnp.float32) * g...  79 us
    another operation x27, local copies, waits for them, and re-layouts, sweep(): jnp.stack(tap_sums)  77.1 us
    add x27, other arithmetic, sweep(): accumulated = accumulated + tap_row[offset] * shifted  73.8 us
    slice x54, local copies, waits for them, and re-layouts, sweep(): accumulated = accumulated + tap_row[offset] * shifted  71.8 us
    all_to_all x3, blocking collectives, scatter_sum(): arrived = lax.all_to_all(parts, axes, 0, 0)  49.8 us
    all_to_all x2, blocking collectives, gathered(): lax.all_to_all(copies, axes, 0, 0).reshape(count * block.shape[0], LANES)  25.9 us
    dynamic_update_slice x27, local copies, waits for them, and re-layouts, sweep(): lax.dynamic_update_index_in_dim(kernel_sums, jnp.stack(tap_sums), row_off...  16.5 us
    ppermute x4, starting transfers between devices, padded_2(): lax.ppermute(lax.slice_in_dim(block, 0, width, axis=dim), axis, backward)  14.3 us
  transfers between devices with their start and end apart: 9, of which 4 were waited for; matrix products, arithmetic and copies ran while one was open for 2% of the time, Pallas kernels for 0%

profile of v1, /device:TPU:1, one launch (start us, length us, event | category | flops | bytes accessed | tf_op | source)
XLA Modules:
  0.0 459.8 jit_solution(3448541404352663519)
XLA Ops:
  2.4 8.7 %collective-permute-start.5 = (bf16[13,16,256]{2,1,0:T(8,128)(2,1)}, bf16[13,16,256]{2,1,0:T(8,128)(2,1)}, u32[]{:S(2)}, u32[]{:S(2)}) collective-permute-start(bf16[13,16,256]{2,1,0:T(8,128)(2,1)} %get-tuple-element.281), channel_id=1, source_target_pairs={{32,0},{64,32},{96,64},{128,96},{160,128},{192,160},{224,192},{256... | collective-permute-start | bytes 319496 | tf_op jit(solution)/shard_map/ppermute | solution.py:27
  16.2 3.0 collective-permute-start.1
  28.4 4.0 collective-permute-start.2
  35.1 3.4 collective-permute-done.7
  38.9 3.1 collective-permute-done.2
  42.0 3.9 collective-permute-done.3
  46.3 318.6 %while.18 = (s32[]{:T(128)}, f32[16,16,256]{2,1,0:T(8,128)S(1)}, bf16[27,27,256]{2,1,0:T(8,128)(2,1)}, f32[27,27,256]{2,1,0:T(8,128)}, bf16[42,42,256]{2,1,0:T(8...) while((s32[]{:T(128)}, f32[16,16,256]{2,1,0:T(8,128)S(1)}, ...), condition=%wide.region_28.29_spmd.clone, body=%wide.region_0.28_spmd.clone.sunk | while | flops 10806561 | bytes 8047621 | solution.py:118
  50.9 2.9 stack.309
  54.8 2.7 multiply_add_fusion.3
  62.6 2.9 stack.309
  66.6 2.7 multiply_add_fusion.3
  74.4 2.9 stack.309
  78.4 2.7 multiply_add_fusion.3
  86.2 2.9 stack.309
  90.2 2.7 multiply_add_fusion.3
  98.0 2.9 stack.309
  101.9 2.7 multiply_add_fusion.3
  109.8 2.9 stack.309
  113.7 2.7 multiply_add_fusion.3
  121.6 2.9 stack.309
  125.5 2.7 multiply_add_fusion.3
  133.4 2.9 stack.309
  137.3 2.7 multiply_add_fusion.3
  145.2 2.9 stack.309
  149.1 2.7 multiply_add_fusion.3
  156.9 2.9 stack.309
  160.9 2.7 multiply_add_fusion.3
  168.7 2.9 stack.309
  172.7 2.7 multiply_add_fusion.3
  180.6 2.9 stack.309
  184.6 2.7 multiply_add_fusion.3
  192.4 2.9 stack.309
  196.4 2.7 multiply_add_fusion.3
  204.2 2.9 stack.309
  208.2 2.7 multiply_add_fusion.3
  216.0 2.9 stack.309
  220.0 2.7 multiply_add_fusion.3
  227.8 2.9 stack.309
  231.7 2.7 multiply_add_fusion.3
  239.6 2.9 stack.309
  243.5 2.7 multiply_add_fusion.3
  251.4 2.9 stack.309
  255.3 2.7 multiply_add_fusion.3
  263.2 2.9 stack.309
  267.1 2.7 multiply_add_fusion.3
  274.9 2.9 stack.309
  278.9 2.7 multiply_add_fusion.3
  286.7 2.9 stack.309
  298.5 2.9 stack.309
  302.5 2.7 multiply_add_fusion.3
  310.3 2.9 stack.309
  322.1 2.9 stack.309
  326.0 2.7 multiply_add_fusion.3
  333.9 2.9 stack.309
  345.7 2.9 stack.309
  349.7 2.7 multiply_add_fusion.3
  357.6 2.9 stack.309
  366.2 5.3 %all_to_all.30 = bf16[2,2816,128]{2,1,0:T(8,128)(2,1)S(1)} all-to-all(bf16[2,2816,128]{2,1,0:T(8,128)(2,1)S(1)} %bitcast.225), channel_id=1, replica_groups=mesh['yh'=2,'x'=4,'core'=2,'yl'=2,'z'=16] {'core'}, dimensions={0} | all-to-all | bytes 2883584 | tf_op jit(solution)/shard_map/all_to_all | solution.py:54
  372.2 23.9 %all_to_all.31 = bf16[16,176,128]{2,1,0:T(8,128)(2,1)S(1)} all-to-all(bf16[16,176,128]{2,1,0:T(8,128)(2,1)S(1)} %bitcast.226), channel_id=1, replica_groups=mesh['yh'=2,'x'=4,'core'=2,'yl'=2,'z'=16] {'x','yh','yl'}, dimensions={0} | all-to-all | bytes 1441792 | tf_op jit(solution)/shard_map/all_to_all | solution.py:54
  396.2 20.7 %all_to_all.32 = f32[16,11,128]{2,1,0:T(8,128)S(1)} all-to-all(f32[16,11,128]{2,1,0:T(8,128)S(1)} %reshape.146), channel_id=1, replica_groups=mesh['yh'=2,'x'=4,'core'=2,'yl'=2,'z'=16] {'z'}, dimensions={0} | all-to-all | bytes 180224 | tf_op jit(solution)/shard_map/all_to_all | solution.py:54
  416.9 16.8 %all_to_all.33 = bf16[16,11,128]{2,1,0:T(8,128)(2,1)S(1)} all-to-all(bf16[16,11,128]{2,1,0:T(8,128)(2,1)S(1)} %broadcast_in_dim.39), channel_id=1, replica_groups=mesh['yh'=2,'x'=4,'core'=2,'yl'=2,'z'=16] {'z'}, dimensions={0} | all-to-all | bytes 90112 | tf_op jit(solution)/shard_map/all_to_all | solution.py:61
  434.7 3.7 all-to-all-start.4
  439.1 9.4 %all-to-all-done.4 = bf16[16,176,128]{2,1,0:T(8,128)(2,1)S(1)} async-done(((bf16[16,176,128]{2,1,0:T(8,128)(2,1)}), bf16[16,176,128]{2,1,0:T(8,128)(2,1)S(1)}, u32[]{:S(2)}, u32[]{:S(2)}) %all-to-all-start.4) | async-done | bytes 720928 | tf_op jit(solution)/shard_map/all_to_all | solution.py:61
  448.6 9.2 %all_to_all.34 = bf16[2,2816,128]{2,1,0:T(8,128)(2,1)S(1)} all-to-all(bf16[2,2816,128]{2,1,0:T(8,128)(2,1)S(1)} %broadcast_in_dim.43), channel_id=1, replica_groups=mesh['yh'=2,'x'=4,'core'=2,'yl'=2,'z'=16] {'core'}, dimensions={0} | all-to-all | bytes 2883584 | tf_op jit(solution)/shard_map/all_to_all | solution.py:61
  (209 shorter events, 203.5 us)
Async XLA Ops:
  0.6 12.4 %copy-start = (bf16[256,1024]{1,0:T(8,128)(2,1)S(1)}, bf16[256,1024]{1,0:T(8,128)(2,1)}, u32[]{:S(2)}) copy-start(bf16[256,1024]{1,0:T(8,128)(2,1)} %param.11) | copy-start | bytes 1572868
  0.6 13.6 %copy-start.10 = (bf16[1024,256]{1,0:T(8,128)(2,1)S(1)}, bf16[1024,256]{1,0:T(8,128)(2,1)}, u32[]{:S(2)}) copy-start(bf16[1024,256]{1,0:T(8,128)(2,1)} %param.12) | copy-start | bytes 1572868
  0.7 13.6 %copy-start.9 = (bf16[16,16,256]{2,1,0:T(8,128)(2,1)S(1)}, bf16[16,16,256]{2,1,0:T(8,128)(2,1)}, u32[]{:S(2)}) copy-start(bf16[16,16,256]{2,1,0:T(8,128)(2,1)} %param.10) | copy-start | bytes 393220
  2.4 22.1 %collective-permute-start.5 = (bf16[13,16,256]{2,1,0:T(8,128)(2,1)}, bf16[13,16,256]{2,1,0:T(8,128)(2,1)}, u32[]{:S(2)}, u32[]{:S(2)}) collective-permute-start(bf16[13,16,256]{2,1,0:T(8,128)(2,1)} %get-tuple-element.281), channel_id=1, source_target_pairs={{32,0},{64,32},{96,64},{128,96},{160,128},{192,160},{224,192},{256... | collective-permute-start | bytes 319496 | tf_op jit(solution)/shard_map/ppermute | solution.py:27
  11.1 12.4 %collective-permute-start.4 = (bf16[13,16,256]{2,1,0:T(8,128)(2,1)}, bf16[13,16,256]{2,1,0:T(8,128)(2,1)}, u32[]{:S(2)}, u32[]{:S(2)}) collective-permute-start(bf16[13,16,256]{2,1,0:T(8,128)(2,1)} %get-tuple-element.282), channel_id=1, source_target_pairs={{0,32},{32,64},{64,96},{96,128},{128,160},{160,192},{192,224},{224... | collective-permute-start | bytes 319496 | tf_op jit(solution)/shard_map/ppermute | solution.py:24
  15.1 6.6 %copy-start.3 = (bf16[16,16,256]{2,1,0:T(8,128)(2,1)S(1)}, bf16[16,16,256]{2,1,0:T(8,128)(2,1)}, u32[]{:S(2)}) copy-start(bf16[16,16,256]{2,1,0:T(8,128)(2,1)} %param.9) | copy-start | bytes 393220
  15.1 7.0 %copy-start.4 = (bf16[27,27,256]{2,1,0:T(8,128)(2,1)S(1)}, bf16[27,27,256]{2,1,0:T(8,128)(2,1)}, u32[]{:S(2)}) copy-start(bf16[27,27,256]{2,1,0:T(8,128)(2,1)} %param.13) | copy-start | bytes 1119748
  16.2 12.0 %collective-permute-start.1 = (bf16[13,16,256]{2,1,0:T(8,128)(2,1)}, bf16[13,16,256]{2,1,0:T(8,128)(2,1)S(1)}, u32[]{:S(2)}, u32[]{:S(2)}) collective-permute-start(bf16[13,16,256]{2,1,0:T(8,128)(2,1)} %bitcast.4), channel_id=1, source_target_pairs={{32,0},{64,32},{96,64},{128,96},{160,128},{192,160},{224,192},{256... | collective-permute-start | bytes 319496 | tf_op jit(solution)/shard_map/ppermute | solution.py:27
  19.2 9.0 %collective-permute-start = (bf16[13,16,256]{2,1,0:T(8,128)(2,1)}, bf16[13,16,256]{2,1,0:T(8,128)(2,1)S(1)}, u32[]{:S(2)}, u32[]{:S(2)}) collective-permute-start(bf16[13,16,256]{2,1,0:T(8,128)(2,1)} %bitcast.3), channel_id=1, source_target_pairs={{0,32},{32,64},{64,96},{96,128},{128,160},{160,192},{192,224},{224... | collective-permute-start | bytes 319496 | tf_op jit(solution)/shard_map/ppermute | solution.py:24
  23.1 1.3 copy-start.1
  25.6 9.6 %collective-permute-start.6 = (bf16[42,13,256]{2,1,0:T(8,128)(2,1)S(1)}, bf16[42,13,256]{2,1,0:T(8,128)(2,1)S(1)}, u32[]{:S(2)}, u32[]{:S(2)}) collective-permute-start(bf16[42,13,256]{2,1,0:T(8,128)(2,1)S(1)} %get-tuple-element.277), channel_id=1, source_target_pairs={{0,1},{1,2},{2,3},{3,4},{4,5},{5,6},{6,7},{7,8},{8,9},{9,10},{10,1... | collective-permute-start | bytes 838664 | tf_op jit(solution)/shard_map/ppermute | solution.py:24
  26.9 11.6 %collective-permute-start.7 = (bf16[42,13,256]{2,1,0:T(8,128)(2,1)S(1)}, bf16[42,13,256]{2,1,0:T(8,128)(2,1)S(1)}, u32[]{:S(2)}, u32[]{:S(2)}) collective-permute-start(bf16[42,13,256]{2,1,0:T(8,128)(2,1)S(1)} %get-tuple-element.278), channel_id=1, source_target_pairs={{1,0},{2,1},{3,2},{4,3},{5,4},{6,5},{7,6},{8,7},{9,8},{10,9},{11,1... | collective-permute-start | bytes 838664 | tf_op jit(solution)/shard_map/ppermute | solution.py:27
  28.2 6.9 %copy-start.5 = (bf16[13,16,256]{2,1,0:T(8,128)(2,1)}, bf16[13,16,256]{2,1,0:T(8,128)(2,1)S(1)}, u32[]{:S(2)}) copy-start(bf16[13,16,256]{2,1,0:T(8,128)(2,1)S(1)} %collective-permute-done.1) | copy-start | bytes 319492
  28.2 6.9 %copy-start.7 = (bf16[13,16,256]{2,1,0:T(8,128)(2,1)}, bf16[13,16,256]{2,1,0:T(8,128)(2,1)S(1)}, u32[]{:S(2)}) copy-start(bf16[13,16,256]{2,1,0:T(8,128)(2,1)S(1)} %collective-permute-done) | copy-start | bytes 319492
  28.4 13.6 %collective-permute-start.2 = (bf16[42,13,256]{2,1,0:T(8,128)(2,1)S(1)}, bf16[42,13,256]{2,1,0:T(8,128)(2,1)S(1)}, u32[]{:S(2)}, u32[]{:S(2)}) collective-permute-start(bf16[42,13,256]{2,1,0:T(8,128)(2,1)S(1)} %get-tuple-element.279), channel_id=1, source_target_pairs={{0,1},{1,2},{2,3},{3,4},{4,5},{5,6},{6,7},{7,8},{8,9},{9,10},{10,1... | collective-permute-start | bytes 838664 | tf_op jit(solution)/shard_map/ppermute | solution.py:24
  32.4 13.4 %collective-permute-start.3 = (bf16[42,13,256]{2,1,0:T(8,128)(2,1)S(1)}, bf16[42,13,256]{2,1,0:T(8,128)(2,1)S(1)}, u32[]{:S(2)}, u32[]{:S(2)}) collective-permute-start(bf16[42,13,256]{2,1,0:T(8,128)(2,1)S(1)} %get-tuple-element.280), channel_id=1, source_target_pairs={{1,0},{2,1},{3,2},{4,3},{5,4},{6,5},{7,6},{8,7},{9,8},{10,9},{11,1... | collective-permute-start | bytes 838664 | tf_op jit(solution)/shard_map/ppermute | solution.py:27
  35.1 10.8 %copy-start.6 = (bf16[13,16,256]{2,1,0:T(8,128)(2,1)S(1)}, bf16[13,16,256]{2,1,0:T(8,128)(2,1)}, u32[]{:S(2)}) copy-start(bf16[13,16,256]{2,1,0:T(8,128)(2,1)} %copy-done.5) | copy-start | bytes 319492
  35.1 10.7 %copy-start.8 = (bf16[13,16,256]{2,1,0:T(8,128)(2,1)S(1)}, bf16[13,16,256]{2,1,0:T(8,128)(2,1)}, u32[]{:S(2)}) copy-start(bf16[13,16,256]{2,1,0:T(8,128)(2,1)} %copy-done.7) | copy-start | bytes 319492
  364.9 1.2 copy-start.2
  434.7 13.8 %all-to-all-start.4 = ((bf16[16,176,128]{2,1,0:T(8,128)(2,1)}), bf16[16,176,128]{2,1,0:T(8,128)(2,1)S(1)}, u32[]{:S(2)}, u32[]{:S(2)}) async-start(bf16[16,176,128]{2,1,0:T(8,128)(2,1)} %broadcast_in_dim.41), calls=%async_computation.4 | async-start | bytes 1441792 | tf_op jit(solution)/shard_map/all_to_all | solution.py:61

commit v2 on v1

v2 whole, which is shorter than its diff:
```python
import functools
import math

import jax
import jax.numpy as jnp
import numpy as np
from jax import lax
from jax.experimental import pallas as pl
from jax.experimental.pallas import tpu as pltpu
from jax.sharding import Mesh, PartitionSpec as P

KS = 27
RADIUS = KS // 2
TILE = 16
PATCH = TILE + KS - 1
HALF = PATCH // 2 + 1
BAND = 24
CELLS = 2 * BAND // 8
ROW = ("yh", "x", "core")
COL = ("yl", "z")
PLANE = ("x", "yh", "yl")
LANES = 128


gelu_coef = 0.044715
root_coef = math.sqrt(2.0 / math.pi)


def split_stack(matrix, order):
    high = matrix.astype(jnp.bfloat16)
    low = (matrix - high.astype(np.float64)).astype(jnp.bfloat16)
    return np.concatenate([{"h": high, "l": low}[part] for part in order], axis=1)


def forward_matrix(positions):
    matrix = np.zeros((2 * BAND, len(positions)))
    freq = np.arange(HALF)
    for column, position in enumerate(positions):
        if position is not None:
            angle = 2.0 * np.pi * ((freq * position) % PATCH) / PATCH
            matrix[:HALF, column] = np.cos(angle)
            matrix[BAND : BAND + HALF, column] = -np.sin(angle)
    return split_stack(matrix, "hl")


def inverse_matrix(positions, rows):
    matrix = np.zeros((rows, 2 * BAND))
    freq = np.arange(HALF)
    weight = np.where((freq == 0) | (2 * freq == PATCH), 1.0, 2.0) / PATCH
    for row, position in enumerate(positions):
        angle = 2.0 * np.pi * ((freq * position) % PATCH) / PATCH
        matrix[row, :HALF] = weight * np.cos(angle)
        matrix[row, BAND : BAND + HALF] = -weight * np.sin(angle)
    return split_stack(matrix, "hlh")


PATCH_POSITIONS = [i - TILE + RADIUS if 0 <= i - TILE + RADIUS < PATCH else None for i in range(3 * TILE)]


def transform(matrix_ref, pieces, out_ref, count, unroll):
    def some(step, carry):
        for extra in range(unroll):
            row = step * unroll + extra
            pixels = jnp.concatenate([piece[row] for piece in pieces] * 2, axis=0)
            spectrum = jnp.dot(matrix_ref[...], pixels, preferred_element_type=jnp.float32)
            for lane in range(2):
                part = spectrum[:, lane * LANES : (lane + 1) * LANES]
                out_ref[row, lane * CELLS : (lane + 1) * CELLS] = part.reshape(CELLS, 8, LANES)
        return carry

    lax.fori_loop(0, count // unroll, some, 0)


def back(matrix_ref, spectrum_ref, row):
    lanes = [
        spectrum_ref[row, lane * CELLS : (lane + 1) * CELLS].reshape(2 * BAND, LANES) for lane in range(2)
    ]
    values = jnp.concatenate(lanes, axis=1)
    high = values.astype(jnp.bfloat16)
    low = (values - high.astype(jnp.float32)).astype(jnp.bfloat16)
    stacked = jnp.concatenate([high, high, low], axis=0)
    return jnp.dot(matrix_ref[...], stacked, preferred_element_type=jnp.float32)


def each_cell(work):
    def lane_step(lane, carry):
        def cell_step(cell, inner):
            work(lane * CELLS + cell, lane * CELLS + CELLS // 2 + cell)
            return inner

        return lax.fori_loop(0, CELLS // 2, cell_step, carry)

    lax.fori_loop(0, 2, lane_step, 0)


def taps_kernel(left, centre, right, grad, patch_mat, tile_mat, inv_mat, out_ref, wide, tile, sums):
    transform(patch_mat, [left, centre, right], wide, PATCH, 6)
    transform(tile_mat, [grad], tile, TILE, 4)
    block = 9

    def work(re, im):
        def block_step(index, carry):
            base = index * block
            real = [None] * block
            imag = [None] * block
            for i in range(TILE):
                gr, gi = tile[i, re], tile[i, im]
                for a in range(block):
                    xr, xi = wide[base + i + a, re], wide[base + i + a, im]
                    new_r = xr * gr + xi * gi
                    new_i = xi * gr - xr * gi
                    real[a] = new_r if i == 0 else real[a] + new_r
                    imag[a] = new_i if i == 0 else imag[a] + new_i
            for a in range(block):
                sums[base + a, re] = real[a]
                sums[base + a, im] = imag[a]
            return carry

        lax.fori_loop(0, KS // block, block_step, 0)

    each_cell(work)
    for a in range(KS):
        out_ref[a * KS : (a + 1) * KS, :] = back(inv_mat, sums, a)[:KS]
    out_ref[KS * KS :, :] = jnp.zeros((out_ref.shape[0] - KS * KS, out_ref.shape[1]), jnp.float32)


def conv_kernel(left, centre, right, taps, grad, patch_mat, taps_mat, inv_mat, out_ref, wide, filt, sums):
    transform(patch_mat, [left, centre, right], wide, PATCH, 6)
    transform(taps_mat, [taps], filt, KS, 3)
    block = 8

    def work(re, im):
        def block_step(index, carry):
            base = index * block
            real = [None] * block
            imag = [None] * block
            for a in range(KS):
                kr, ki = filt[a, re], filt[a, im]
                for i in range(block):
                    row = base + i + KS - 1 - a
                    gr, gi = wide[row, re], wide[row, im]
                    new_r = kr * gr - ki * gi
                    new_i = kr * gi + ki * gr
                    real[i] = new_r if a == 0 else real[i] + new_r
                    imag[i] = new_i if a == 0 else imag[i] + new_i
            for i in range(block):
                sums[base + i, re] = real[i]
                sums[base + i, im] = imag[i]
            return carry

        lax.fori_loop(0, TILE // block, block_step, 0)

    each_cell(work)
    for i in range(TILE):
        out_ref[i] = (grad[i].astype(jnp.float32) + back(inv_mat, sums, i)).astype(jnp.bfloat16)


def spectral_call(kernel, out_shape, second_rows, sum_rows, args):
    channels = args[0].shape[-1]
    return pl.pallas_call(
        kernel,
        out_shape=out_shape,
        in_specs=[pl.BlockSpec(memory_space=pltpu.VMEM)] * len(args),
        out_specs=pl.BlockSpec(memory_space=pltpu.VMEM),
        scratch_shapes=[
            pltpu.VMEM((PATCH, 2 * CELLS, 8, LANES), jnp.float32),
            pltpu.VMEM((second_rows, 2 * CELLS, 8, LANES), jnp.float32),
            pltpu.VMEM((sum_rows, 2 * CELLS, 8, LANES), jnp.float32),
        ],
        compiler_params=pltpu.CompilerParams(vmem_limit_bytes=32 << 20),
        cost_estimate=pl.CostEstimate(flops=4_000_000_000, bytes_accessed=8_000_000, transcendentals=0),
    )(*args)


def taps_gradient(sides, grad_tile):
    mats = (
        forward_matrix(PATCH_POSITIONS),
        forward_matrix(list(range(TILE))),
        inverse_matrix(range(KS), 32),
    )
    args = (*sides, grad_tile, *(jnp.asarray(m) for m in mats))
    out = jax.ShapeDtypeStruct((768, grad_tile.shape[-1]), jnp.float32)
    return spectral_call(taps_kernel, out, TILE, KS, args)


def conv_backward(sides, taps, grad_tile):
    mats = (
        forward_matrix(PATCH_POSITIONS),
        forward_matrix(list(range(KS)) + [None] * 5),
        inverse_matrix(range(KS - 1, PATCH), TILE),
    )
    padded = jnp.pad(taps, ((0, 0), (0, 32 - KS), (0, 0)))
    args = (*sides, padded, grad_tile, *(jnp.asarray(m) for m in mats))
    out = jax.ShapeDtypeStruct(grad_tile.shape, jnp.bfloat16)
    return spectral_call(conv_kernel, out, KS, TILE, args)


def shifted(block, axes, step):
    count = lax.axis_size(axes)
    pairs = [(i, i + step) for i in range(count) if 0 <= i + step < count]
    return lax.ppermute(block, axes, pairs)


def halo(block):
    low = shifted(block[-RADIUS:], ROW, 1)
    high = shifted(block[:RADIUS], ROW, -1)
    tall = jnp.concatenate([low, block, high], axis=0)
    return (shifted(tall, COL, 1), tall, shifted(tall, COL, -1))


def gelu_parts(values):
    tanh_part = jnp.tanh(root_coef * (values + gelu_coef * values * values * values))
    result = 0.5 * values * (1.0 + tanh_part)
    slopes = 0.5 * (1.0 + tanh_part) + 0.5 * values * (1.0 - tanh_part * tanh_part) * root_coef * (
        1.0 + 3.0 * gelu_coef * values * values
    )
    return (result, slopes)


def to_rows(block):
    rows, cols = block.shape
    return block.reshape(rows // 8, 8, cols // LANES, LANES).transpose(0, 2, 1, 3).reshape(-1, LANES)


def from_rows(flat, shape):
    rows, cols = shape
    return flat.reshape(rows // 8, cols // LANES, 8, LANES).transpose(0, 2, 1, 3).reshape(rows, cols)


def scatter_sum(block, axes):
    count = lax.axis_size(axes)
    parts = block.reshape(count, block.shape[0] // count, LANES)
    arrived = lax.all_to_all(parts, axes, 0, 0)
    return jnp.sum(arrived.astype(jnp.float32), axis=0)


def gathered(block, axes):
    count = lax.axis_size(axes)
    copies = jnp.broadcast_to(block[None], (count,) + block.shape)
    return lax.all_to_all(copies, axes, 0, 0).reshape(count * block.shape[0], LANES)


def summed(blocks, scale):
    flat = jnp.concatenate([to_rows(block.astype(jnp.bfloat16)) for block in blocks], axis=0)
    half = scatter_sum(flat, "core")
    part = scatter_sum(half.astype(jnp.bfloat16), PLANE)
    total = (scatter_sum(part, "z") * scale).astype(jnp.bfloat16)
    return gathered(gathered(gathered(total, "z"), PLANE), "core")


def per_device(inputs, stored, upstream, weight_in, weight_out, kernel):
    tile_rows, tile_cols, channels = stored.shape
    sides_in = halo(inputs)
    flat_z = stored.reshape(tile_rows * tile_cols, channels)
    flat_g = upstream.reshape(tile_rows * tile_cols, channels)
    hidden = jnp.dot(flat_z, weight_in, preferred_element_type=jnp.float32)
    values, slopes = gelu_parts(hidden)
    active = values.astype(jnp.bfloat16)
    back_proj = jnp.einsum("nc,fc->nf", flat_g, weight_out, preferred_element_type=jnp.float32)
    grad_hidden = (back_proj * slopes).astype(jnp.bfloat16)
    grad_flat = (
        flat_g.astype(jnp.float32)
        + jnp.einsum("nf,cf->nc", grad_hidden, weight_in, preferred_element_type=jnp.float32)
    ).astype(jnp.bfloat16)
    sum_in = jnp.einsum("nc,nf->cf", flat_z, grad_hidden, preferred_element_type=jnp.float32)
    sum_out = jnp.einsum("nf,nc->fc", active, flat_g, preferred_element_type=jnp.float32)
    grad_mid = grad_flat.reshape(tile_rows, tile_cols, channels)
    tap_sums = taps_gradient(sides_in, grad_mid)
    sides_mid = halo(grad_mid)
    grad_inputs = conv_backward(sides_mid, kernel, grad_mid)
    pixel_count = tile_rows * tile_cols * lax.axis_size(ROW) * lax.axis_size(COL)
    grad_scale = 1.0 / math.sqrt(pixel_count)
    final = summed([sum_in, sum_out, tap_sums], grad_scale)
    rows_in = sum_in.size // LANES
    final_in = from_rows(final[:rows_in], sum_in.shape)
    final_out = from_rows(final[rows_in : 2 * rows_in], sum_out.shape)
    final_kernel = from_rows(final[2 * rows_in :], tap_sums.shape)[: KS * KS].reshape(KS, KS, channels)
    return (grad_inputs, final_in, final_out, final_kernel)


def solution(mesh):
    fine = Mesh(mesh.devices.reshape(2, 4, 2, 2, 16), ("yh", "x", "core", "yl", "z"))
    return jax.shard_map(
        per_device,
        mesh=fine,
        in_specs=(P(ROW, COL, None), P(ROW, COL, None), P(ROW, COL, None), P(), P(), P()),
        out_specs=(P(ROW, COL, None), P(), P(), P()),
        check_vma=False,
    )
```

time: 466 us -> 132 us (0.28); the launches traced: 460 us -> 131 us
  local copies, waits for them, and re-layouts: 175 us -> 7.66 us
  other arithmetic: 156 us -> 1.04 us
  blocking collectives: 75.7 us -> 40.2 us
  starting transfers between devices: 27.8 us -> 44.5 us
  Pallas kernels: 0 us -> 12.4 us
    reduce_sum x54 -> x0, other arithmetic: 79 us -> none  [sweep(): jnp.sum(source_rows[:, offset:offset + tile_cols].astype(jnp.float32) * g...]
    another operation x27 -> x0, local copies, waits for them, and re-layouts: 77.1 us -> none  [sweep(): jnp.stack(tap_sums)]
    add x27 -> x0, other arithmetic: 73.8 us -> none  [sweep(): accumulated = accumulated + tap_row[offset] * shifted]
    slice x59 -> x3, local copies, waits for them, and re-layouts: 74.6 us -> 1.1 us  [the longest x1 1.05 us: halo(): high = shifted(block[:RADIUS], ROW, -1)]
    all_to_all x2 -> x1, blocking collectives: 25.9 us -> 7.03 us  [gathered(): lax.all_to_all(copies, axes, 0, 0).reshape(count * block.shape[0], LANES)]
    all_to_all x3 -> x2, blocking collectives: 49.8 us -> 33.1 us  [scatter_sum(): arrived = lax.all_to_all(parts, axes, 0, 0)]
    dynamic_update_slice x27 -> x0, local copies, waits for them, and re-layouts: 16.5 us -> none  [sweep(): lax.dynamic_update_index_in_dim(kernel_sums, jnp.stack(tap_sums), row_off...]
    pallas_call x0 -> x2, Pallas kernels: none -> 12.4 us  [spectral_call(): pl.pallas_call(kernel, out_shape=out_shape, in_specs=[pl.BlockSpec(memory...]
  transfers between devices with their start and end apart: 9 -> 11, of which waited for: 4 -> 5; matrix products, arithmetic and copies ran while one was open for 2% -> 4% of each run, Pallas kernels for 0% -> 5%
where the time goes in v2:
time: 132 us; the launch traced here: 131 us
  starting transfers between devices  44.5 us (34%)
  blocking collectives  40.2 us (30%)
  waiting for transfers between devices  21.3 us (16%)
  Pallas kernels  12.4 us (9%)
  local copies, waits for them, and re-layouts  7.66 us (6%)
  matrix products  3.28 us (2%)
    all_to_all x2, blocking collectives, scatter_sum(): arrived = lax.all_to_all(parts, axes, 0, 0)  33.1 us
    ppermute x8, starting transfers between devices, shifted(): return lax.ppermute(block, axes, pairs)  27.4 us
    pallas_call x2, Pallas kernels, spectral_call(): pl.pallas_call(kernel, out_shape=out_shape, in_specs=[pl.BlockSpec(memory...  12.4 us
    all_to_all x2, starting transfers between devices, gathered(): lax.all_to_all(copies, axes, 0, 0).reshape(count * block.shape[0], LANES)  11.8 us
    all_to_all x2, waiting for transfers between devices, gathered(): lax.all_to_all(copies, axes, 0, 0).reshape(count * block.shape[0], LANES)  11.1 us
    all_to_all x1, blocking collectives, gathered(): lax.all_to_all(copies, axes, 0, 0).reshape(count * block.shape[0], LANES)  7.03 us
    all_to_all x1, waiting for transfers between devices, scatter_sum(): arrived = lax.all_to_all(parts, axes, 0, 0)  5.95 us
    all_to_all x1, starting transfers between devices, scatter_sum(): arrived = lax.all_to_all(parts, axes, 0, 0)  5.35 us
  transfers between devices with their start and end apart: 11, of which 5 were waited for; matrix products, arithmetic and copies ran while one was open for 4% of the time, Pallas kernels for 5%

profile of v2, /device:TPU:1, one launch (start us, length us, event | category | flops | bytes accessed | tf_op | source)
XLA Modules:
  0.0 131.3 jit_solution(17854147999195986472)
XLA Ops:
  0.6 0.0 copy-start
  0.6 0.0 copy-start.12
  0.7 0.0 copy-start.11
  0.7 1.1 fusion.17
  1.7 8.7 %collective-permute-start.5 = (bf16[13,16,256]{2,1,0:T(8,128)(2,1)S(1)}, bf16[13,16,256]{2,1,0:T(8,128)(2,1)S(1)}, u32[]{:S(2)}, u32[]{:S(2)}) collective-permute-start(bf16[13,16,256]{2,1,0:T(8,128)(2,1)S(1)} %get-tuple-element.6), channel_id=1, source_target_pairs={{32,0},{64,32},{96,64},{128,96},{160,128},{192,160},{224,192},{256... | collective-permute-start | bytes 319496 | tf_op jit(solution)/shard_map/ppermute | solution.py:201
  10.5 1.9 %collective-permute-start.4 = (bf16[13,16,256]{2,1,0:T(8,128)(2,1)S(1)}, bf16[13,16,256]{2,1,0:T(8,128)(2,1)S(1)}, u32[]{:S(2)}, u32[]{:S(2)}) collective-permute-start(bf16[13,16,256]{2,1,0:T(8,128)(2,1)S(1)} %get-tuple-element.7), channel_id=1, source_target_pairs={{0,32},{32,64},{64,96},{96,128},{128,160},{160,192},{192,224},{224... | collective-permute-start | bytes 319496 | tf_op jit(solution)/shard_map/ppermute | solution.py:201
  12.4 0.0 copy-done
  12.4 1.2 fusion.19
  13.6 0.0 copy-start.6
  13.6 0.0 copy-done.12
  13.6 0.0 copy-done.11
  13.7 0.8 fusion
  14.5 0.2 copy-done.6
  14.6 0.3 fusion.2
  15.0 0.0 collective-permute-done.4
  15.0 0.5 copy-done.8
  15.5 0.0 collective-permute-done.5
  15.6 1.3 collective-permute-start.7
  16.9 4.0 %collective-permute-start.6 = (bf16[42,16,256]{2,1,0:T(8,128)(2,1)S(1)}, bf16[42,16,256]{2,1,0:T(8,128)(2,1)S(1)}, u32[]{:S(2)}, u32[]{:S(2)}) collective-permute-start(bf16[42,16,256]{2,1,0:T(8,128)(2,1)S(1)} %constant_dynamic-update-slice_fusion.centre), channel_id=1, source_target_pairs={{0,1},{1,2},{2,3},{3,4},{4,5},{5,6},{6,7},{7,8},{8,9},{9,10},{10,1... | collective-permute-start | bytes 1032200 | tf_op jit(solution)/shard_map/ppermute | solution.py:201
  20.9 0.0 copy-done.9
  20.9 0.4 fusion.1
  21.3 0.2 copy.18
  21.5 0.0 copy-start.7
  21.5 0.1 copy.22
  21.6 0.1 copy.19
  21.7 1.0 copy-done.7
  22.7 0.6 convolution_convert_fusion
  23.3 3.3 %collective-permute-done.7.right = bf16[42,16,256]{2,1,0:T(8,128)(2,1)S(1)} collective-permute-done((bf16[42,16,256]{2,1,0:T(8,128)(2,1)S(1)}, bf16[42,16,256]{2,1,0:T(8,128)(2,1)S(1)}, u32[]{:S(2)}, u32[]{:S(2)}) %collective-permute-start.7) | collective-permute-done | bytes 344096 | tf_op jit(solution)/shard_map/ppermute | solution.py:201
  26.6 0.9 collective-permute-done.6.left
  27.5 0.0 copy-done.1
  27.5 0.0 copy-done.2
  27.5 0.0 copy-done.4
  27.5 5.4 %shard_map.148 = f32[768,256]{1,0:T(8,128)S(1)} custom-call(bf16[42,16,256]{2,1,0:T(8,128)(2,1)S(1)} %collective-permute-done.6.left, bf16[42,16,256]{2,1,0:T(8,128)(2,1)S(1)} %constant_dynamic-update-slice_fusion.centre, bf16[42,16,256]{2,1,0:T(8,128)(2,1)S(1)} %collective-permute-done.7.right, bf16[16,16,256]{2,1,0:T(8,128)(2,1)S(1)} %bitcast.54, ...), custom_call_target="tpu_custom_call" | custom-call | flops 4000000000 | bytes 8000000 | tf_op jit(solution)/shard_map/pallas_call | solution.py:160
  32.9 0.1 pad_maximum_fusion
  33.0 6.2 %all_to_all.30 = bf16[2,2816,128]{2,1,0:T(8,128)(2,1)S(1)} all-to-all(bf16[2,2816,128]{2,1,0:T(8,128)(2,1)S(1)} %bitcast.59), channel_id=1, replica_groups=mesh['yh'=2,'x'=4,'core'=2,'yl'=2,'z'=16] {'core'}, dimensions={0} | all-to-all | bytes 2883584 | tf_op jit(solution)/shard_map/all_to_all | solution.py:233
  39.2 0.7 reduce_sum.30
  39.9 27.0 %all_to_all.31 = bf16[16,176,128]{2,1,0:T(8,128)(2,1)S(1)} all-to-all(bf16[16,176,128]{2,1,0:T(8,128)(2,1)S(1)} %bitcast.60), channel_id=1, replica_groups=mesh['yh'=2,'x'=4,'core'=2,'yl'=2,'z'=16] {'x','yh','yl'}, dimensions={0} | all-to-all | bytes 1441792 | tf_op jit(solution)/shard_map/all_to_all | solution.py:233
  66.9 0.1 convert_reduce_fusion
  67.0 0.7 reshape.87
  67.6 5.4 %all-to-all-start.2 = ((f32[16,11,128]{2,1,0:T(8,128)}), f32[16,11,128]{2,1,0:T(8,128)S(1)}, u32[]{:S(2)}, u32[]{:S(2)}) async-start(f32[16,11,128]{2,1,0:T(8,128)} %reshape.87), calls=%async_computation.2 | async-start | bytes 262144 | tf_op jit(solution)/shard_map/all_to_all | solution.py:233
  73.0 4.1 %collective-permute-start.1 = (bf16[13,16,256]{2,1,0:T(8,128)(2,1)S(1)}, bf16[13,16,256]{2,1,0:T(8,128)(2,1)S(1)}, u32[]{:S(2)}, u32[]{:S(2)}) collective-permute-start(bf16[13,16,256]{2,1,0:T(8,128)(2,1)S(1)} %bitcast.76), channel_id=1, source_target_pairs={{32,0},{64,32},{96,64},{128,96},{160,128},{192,160},{224,192},{256... | collective-permute-start | bytes 319496 | tf_op jit(solution)/shard_map/ppermute | solution.py:201
  77.1 1.9 %collective-permute-start = (bf16[13,16,256]{2,1,0:T(8,128)(2,1)S(1)}, bf16[13,16,256]{2,1,0:T(8,128)(2,1)S(1)}, u32[]{:S(2)}, u32[]{:S(2)}) collective-permute-start(bf16[13,16,256]{2,1,0:T(8,128)(2,1)S(1)} %bitcast.75), channel_id=1, source_target_pairs={{0,32},{32,64},{64,96},{96,128},{128,160},{160,192},{192,224},{224... | collective-permute-start | bytes 319496 | tf_op jit(solution)/shard_map/ppermute | solution.py:201
  79.0 5.9 %all-to-all-done.2 = f32[16,11,128]{2,1,0:T(8,128)S(1)} async-done(((f32[16,11,128]{2,1,0:T(8,128)}), f32[16,11,128]{2,1,0:T(8,128)S(1)}, u32[]{:S(2)}, u32[]{:S(2)}) %all-to-all-start.2) | async-done | bytes 90144 | tf_op jit(solution)/shard_map/all_to_all | solution.py:233
  85.0 0.6 broadcast_in_dim.20
  85.6 5.8 %all-to-all-start.3 = ((bf16[16,11,128]{2,1,0:T(8,128)(2,1)}), bf16[16,11,128]{2,1,0:T(8,128)(2,1)S(1)}, u32[]{:S(2)}, u32[]{:S(2)}) async-start(bf16[16,11,128]{2,1,0:T(8,128)(2,1)} %broadcast_in_dim.20), calls=%async_computation.3 | async-start | bytes 131072 | tf_op jit(solution)/shard_map/all_to_all | solution.py:240
  91.4 0.0 copy-start.10
  91.5 0.0 collective-permute-done.1
  91.5 0.0 collective-permute-done
  91.5 1.4 %collective-permute-start.3 = (bf16[42,16,256]{2,1,0:T(8,128)(2,1)S(1)}, bf16[42,16,256]{2,1,0:T(8,128)(2,1)S(1)}, u32[]{:S(2)}, u32[]{:S(2)}) collective-permute-start(bf16[42,16,256]{2,1,0:T(8,128)(2,1)S(1)} %pad_maximum_fusion.1.centre), channel_id=1, source_target_pairs={{1,0},{2,1},{3,2},{4,3},{5,4},{6,5},{7,6},{8,7},{9,8},{10,9},{11,1... | collective-permute-start | bytes 1032200 | tf_op jit(solution)/shard_map/ppermute | solution.py:201
  93.0 4.0 %collective-permute-start.2 = (bf16[42,16,256]{2,1,0:T(8,128)(2,1)S(1)}, bf16[42,16,256]{2,1,0:T(8,128)(2,1)S(1)}, u32[]{:S(2)}, u32[]{:S(2)}) collective-permute-start(bf16[42,16,256]{2,1,0:T(8,128)(2,1)S(1)} %pad_maximum_fusion.1.centre), channel_id=1, source_target_pairs={{0,1},{1,2},{2,3},{3,4},{4,5},{5,6},{6,7},{7,8},{8,9},{9,10},{10,1... | collective-permute-start | bytes 1032200 | tf_op jit(solution)/shard_map/ppermute | solution.py:201
  97.0 6.1 %all-to-all-done.3 = bf16[16,11,128]{2,1,0:T(8,128)(2,1)S(1)} async-done(((bf16[16,11,128]{2,1,0:T(8,128)(2,1)}), bf16[16,11,128]{2,1,0:T(8,128)(2,1)S(1)}, u32[]{:S(2)}, u32[]{:S(2)}) %all-to-all-start.3) | async-done | bytes 45088 | tf_op jit(solution)/shard_map/all_to_all | solution.py:240
  103.1 0.0 copy-start.3
  103.2 0.0 copy-start.5
  103.2 1.0 broadcast_in_dim.22
  104.1 6.0 %all-to-all-start.4 = ((bf16[16,176,128]{2,1,0:T(8,128)(2,1)}), bf16[16,176,128]{2,1,0:T(8,128)(2,1)S(1)}, u32[]{:S(2)}, u32[]{:S(2)}) async-start(bf16[16,176,128]{2,1,0:T(8,128)(2,1)} %broadcast_in_dim.22), calls=%async_computation.4 | async-start | bytes 1441792 | tf_op jit(solution)/shard_map/all_to_all | solution.py:240
  110.1 0.0 copy-done.10
  110.2 0.0 collective-permute-done.3.right
  110.2 0.0 collective-permute-done.2.left
  110.2 7.0 %shard_map.147 = bf16[16,16,256]{2,1,0:T(8,128)(2,1)} custom-call(bf16[42,16,256]{2,1,0:T(8,128)(2,1)S(1)} %collective-permute-done.2.left, bf16[42,16,256]{2,1,0:T(8,128)(2,1)S(1)} %pad_maximum_fusion.1.centre, bf16[42,16,256]{2,1,0:T(8,128)(2,1)S(1)} %collective-permute-done.3.right, bf16[27,32,256]{2,1,0:T(8,128)(2,1)S(1)} %pad.4.taps, ...), custom_call_target="tpu_custom_call" | custom-call | flops 4000000000 | bytes 8000000 | tf_op jit(solution)/shard_map/pallas_call | solution.py:160
  117.3 5.0 %all-to-all-done.4 = bf16[16,176,128]{2,1,0:T(8,128)(2,1)S(1)} async-done(((bf16[16,176,128]{2,1,0:T(8,128)(2,1)}), bf16[16,176,128]{2,1,0:T(8,128)(2,1)S(1)}, u32[]{:S(2)}, u32[]{:S(2)}) %all-to-all-start.4) | async-done | bytes 720928 | tf_op jit(solution)/shard_map/all_to_all | solution.py:240
  122.2 0.1 broadcast_in_dim.24
  122.3 7.0 %all_to_all.32 = bf16[2,2816,128]{2,1,0:T(8,128)(2,1)S(1)} all-to-all(bf16[2,2816,128]{2,1,0:T(8,128)(2,1)S(1)} %broadcast_in_dim.24), channel_id=1, replica_groups=mesh['yh'=2,'x'=4,'core'=2,'yl'=2,'z'=16] {'core'}, dimensions={0} | all-to-all | bytes 2883584 | tf_op jit(solution)/shard_map/all_to_all | solution.py:240
  129.4 1.0 fusion.16
  130.4 0.9 reshape.95
  (19 shorter events, 0.3 us)
Async XLA Ops:
  0.6 11.8 %copy-start = (bf16[256,1024]{1,0:T(8,128)(2,1)S(1)}, bf16[256,1024]{1,0:T(8,128)(2,1)}, u32[]{:S(2)}) copy-start(bf16[256,1024]{1,0:T(8,128)(2,1)} %param.15) | copy-start | bytes 1572868
  0.6 13.0 %copy-start.12 = (bf16[1024,256]{1,0:T(8,128)(2,1)S(1)}, bf16[1024,256]{1,0:T(8,128)(2,1)}, u32[]{:S(2)}) copy-start(bf16[1024,256]{1,0:T(8,128)(2,1)} %param.16) | copy-start | bytes 1572868
  0.7 13.0 %copy-start.11 = (bf16[16,16,256]{2,1,0:T(8,128)(2,1)S(1)}, bf16[16,16,256]{2,1,0:T(8,128)(2,1)}, u32[]{:S(2)}) copy-start(bf16[16,16,256]{2,1,0:T(8,128)(2,1)} %param.14) | copy-start | bytes 393220
  1.7 13.8 %collective-permute-start.5 = (bf16[13,16,256]{2,1,0:T(8,128)(2,1)S(1)}, bf16[13,16,256]{2,1,0:T(8,128)(2,1)S(1)}, u32[]{:S(2)}, u32[]{:S(2)}) collective-permute-start(bf16[13,16,256]{2,1,0:T(8,128)(2,1)S(1)} %get-tuple-element.6), channel_id=1, source_target_pairs={{32,0},{64,32},{96,64},{128,96},{160,128},{192,160},{224,192},{256... | collective-permute-start | bytes 319496 | tf_op jit(solution)/shard_map/ppermute | solution.py:201
  10.5 4.5 %collective-permute-start.4 = (bf16[13,16,256]{2,1,0:T(8,128)(2,1)S(1)}, bf16[13,16,256]{2,1,0:T(8,128)(2,1)S(1)}, u32[]{:S(2)}, u32[]{:S(2)}) collective-permute-start(bf16[13,16,256]{2,1,0:T(8,128)(2,1)S(1)} %get-tuple-element.7), channel_id=1, source_target_pairs={{0,32},{32,64},{64,96},{96,128},{128,160},{160,192},{192,224},{224... | collective-permute-start | bytes 319496 | tf_op jit(solution)/shard_map/ppermute | solution.py:201
  13.6 1.0 copy-start.6
  14.6 0.9 copy-start.8
  14.6 6.3 %copy-start.9 = (bf16[16,16,256]{2,1,0:T(8,128)(2,1)S(1)}, bf16[16,16,256]{2,1,0:T(8,128)(2,1)}, u32[]{:S(2)}) copy-start(bf16[16,16,256]{2,1,0:T(8,128)(2,1)} %param.13) | copy-start | bytes 393220
  15.6 11.0 %collective-permute-start.7 = (bf16[42,16,256]{2,1,0:T(8,128)(2,1)S(1)}, bf16[42,16,256]{2,1,0:T(8,128)(2,1)S(1)}, u32[]{:S(2)}, u32[]{:S(2)}) collective-permute-start(bf16[42,16,256]{2,1,0:T(8,128)(2,1)S(1)} %constant_dynamic-update-slice_fusion.centre), channel_id=1, source_target_pairs={{1,0},{2,1},{3,2},{4,3},{5,4},{6,5},{7,6},{8,7},{9,8},{10,9},{11,1... | collective-permute-start | bytes 1032200 | tf_op jit(solution)/shard_map/ppermute | solution.py:201
  16.9 10.6 %collective-permute-start.6 = (bf16[42,16,256]{2,1,0:T(8,128)(2,1)S(1)}, bf16[42,16,256]{2,1,0:T(8,128)(2,1)S(1)}, u32[]{:S(2)}, u32[]{:S(2)}) collective-permute-start(bf16[42,16,256]{2,1,0:T(8,128)(2,1)S(1)} %constant_dynamic-update-slice_fusion.centre), channel_id=1, source_target_pairs={{0,1},{1,2},{2,3},{3,4},{4,5},{5,6},{6,7},{7,8},{8,9},{9,10},{10,1... | collective-permute-start | bytes 1032200 | tf_op jit(solution)/shard_map/ppermute | solution.py:201
  21.5 1.2 copy-start.7
  22.7 4.8 %copy-start.1 = (bf16[32,144]{1,0:T(8,128)(2,1)S(1)}, bf16[32,144]{1,0:T(8,128)(2,1)}, u32[]{:S(2)}) copy-start(bf16[32,144]{1,0:T(8,128)(2,1)} %constant.30.clone.inv_mat) | copy-start | bytes 27652
  22.7 4.8 %copy-start.2 = (bf16[48,96]{1,0:T(8,128)(2,1)S(1)}, bf16[48,96]{1,0:T(8,128)(2,1)}, u32[]{:S(2)}) copy-start(bf16[48,96]{1,0:T(8,128)(2,1)} %constant.28.clone.patch_mat) | copy-start | bytes 27652
  22.7 4.8 %copy-start.4 = (bf16[48,32]{1,0:T(8,128)(2,1)S(1)}, bf16[48,32]{1,0:T(8,128)(2,1)}, u32[]{:S(2)}) copy-start(bf16[48,32]{1,0:T(8,128)(2,1)} %constant.29.clone.tile_mat) | copy-start | bytes 9220
  67.6 17.3 %all-to-all-start.2 = ((f32[16,11,128]{2,1,0:T(8,128)}), f32[16,11,128]{2,1,0:T(8,128)S(1)}, u32[]{:S(2)}, u32[]{:S(2)}) async-start(f32[16,11,128]{2,1,0:T(8,128)} %reshape.87), calls=%async_computation.2 | async-start | bytes 262144 | tf_op jit(solution)/shard_map/all_to_all | solution.py:233
  73.0 18.4 %collective-permute-start.1 = (bf16[13,16,256]{2,1,0:T(8,128)(2,1)S(1)}, bf16[13,16,256]{2,1,0:T(8,128)(2,1)S(1)}, u32[]{:S(2)}, u32[]{:S(2)}) collective-permute-start(bf16[13,16,256]{2,1,0:T(8,128)(2,1)S(1)} %bitcast.76), channel_id=1, source_target_pairs={{32,0},{64,32},{96,64},{128,96},{160,128},{192,160},{224,192},{256... | collective-permute-start | bytes 319496 | tf_op jit(solution)/shard_map/ppermute | solution.py:201
  77.1 14.4 %collective-permute-start = (bf16[13,16,256]{2,1,0:T(8,128)(2,1)S(1)}, bf16[13,16,256]{2,1,0:T(8,128)(2,1)S(1)}, u32[]{:S(2)}, u32[]{:S(2)}) collective-permute-start(bf16[13,16,256]{2,1,0:T(8,128)(2,1)S(1)} %bitcast.75), channel_id=1, source_target_pairs={{0,32},{32,64},{64,96},{96,128},{128,160},{160,192},{192,224},{224... | collective-permute-start | bytes 319496 | tf_op jit(solution)/shard_map/ppermute | solution.py:201
  85.6 17.5 %all-to-all-start.3 = ((bf16[16,11,128]{2,1,0:T(8,128)(2,1)}), bf16[16,11,128]{2,1,0:T(8,128)(2,1)S(1)}, u32[]{:S(2)}, u32[]{:S(2)}) async-start(bf16[16,11,128]{2,1,0:T(8,128)(2,1)} %broadcast_in_dim.20), calls=%async_computation.3 | async-start | bytes 131072 | tf_op jit(solution)/shard_map/all_to_all | solution.py:240
  91.4 18.7 %copy-start.10 = (bf16[27,27,256]{2,1,0:T(8,128)(2,1)S(1)}, bf16[27,27,256]{2,1,0:T(8,128)(2,1)}, u32[]{:S(2)}) copy-start(bf16[27,27,256]{2,1,0:T(8,128)(2,1)} %param.17) | copy-start | bytes 1119748
  91.5 18.7 %collective-permute-start.3 = (bf16[42,16,256]{2,1,0:T(8,128)(2,1)S(1)}, bf16[42,16,256]{2,1,0:T(8,128)(2,1)S(1)}, u32[]{:S(2)}, u32[]{:S(2)}) collective-permute-start(bf16[42,16,256]{2,1,0:T(8,128)(2,1)S(1)} %pad_maximum_fusion.1.centre), channel_id=1, source_target_pairs={{1,0},{2,1},{3,2},{4,3},{5,4},{6,5},{7,6},{8,7},{9,8},{10,9},{11,1... | collective-permute-start | bytes 1032200 | tf_op jit(solution)/shard_map/ppermute | solution.py:201
  93.0 17.3 %collective-permute-start.2 = (bf16[42,16,256]{2,1,0:T(8,128)(2,1)S(1)}, bf16[42,16,256]{2,1,0:T(8,128)(2,1)S(1)}, u32[]{:S(2)}, u32[]{:S(2)}) collective-permute-start(bf16[42,16,256]{2,1,0:T(8,128)(2,1)S(1)} %pad_maximum_fusion.1.centre), channel_id=1, source_target_pairs={{0,1},{1,2},{2,3},{3,4},{4,5},{5,6},{6,7},{7,8},{8,9},{9,10},{10,1... | collective-permute-start | bytes 1032200 | tf_op jit(solution)/shard_map/ppermute | solution.py:201
  103.1 7.1 %copy-start.3 = (bf16[48,64]{1,0:T(8,128)(2,1)S(1)}, bf16[48,64]{1,0:T(8,128)(2,1)}, u32[]{:S(2)}) copy-start(bf16[48,64]{1,0:T(8,128)(2,1)} %constant.31.clone.taps_mat) | copy-start | bytes 18436
  103.2 7.1 %copy-start.5 = (bf16[16,144]{1,0:T(8,128)(2,1)S(1)}, bf16[16,144]{1,0:T(8,128)(2,1)}, u32[]{:S(2)}) copy-start(bf16[16,144]{1,0:T(8,128)(2,1)} %constant.32.clone.inv_mat) | copy-start | bytes 13828
  104.1 18.1 %all-to-all-start.4 = ((bf16[16,176,128]{2,1,0:T(8,128)(2,1)}), bf16[16,176,128]{2,1,0:T(8,128)(2,1)S(1)}, u32[]{:S(2)}, u32[]{:S(2)}) async-start(bf16[16,176,128]{2,1,0:T(8,128)(2,1)} %broadcast_in_dim.22), calls=%async_computation.4 | async-start | bytes 1441792 | tf_op jit(solution)/shard_map/all_to_all | solution.py:240

commit v3 on v2

--- a/solution.py
+++ b/solution.py
@@ -1,4 +1,3 @@
-import functools
 import math
 
 import jax
@@ -57,18 +56,24 @@
 PATCH_POSITIONS = [i - TILE + RADIUS if 0 <= i - TILE + RADIUS < PATCH else None for i in range(3 * TILE)]
 
 
-def transform(matrix_ref, pieces, out_ref, count, unroll):
+def transform(matrix_ref, pixels_ref, out_ref, first, unroll):
     def some(step, carry):
         for extra in range(unroll):
             row = step * unroll + extra
-            pixels = jnp.concatenate([piece[row] for piece in pieces] * 2, axis=0)
+            pixels = jnp.concatenate([pixels_ref[row]] * 2, axis=0)
             spectrum = jnp.dot(matrix_ref[...], pixels, preferred_element_type=jnp.float32)
             for lane in range(2):
                 part = spectrum[:, lane * LANES : (lane + 1) * LANES]
-                out_ref[row, lane * CELLS : (lane + 1) * CELLS] = part.reshape(CELLS, 8, LANES)
+                out_ref[first + row, lane * CELLS : (lane + 1) * CELLS] = part.reshape(CELLS, 8, LANES)
         return carry
 
-    lax.fori_loop(0, count // unroll, some, 0)
+    lax.fori_loop(0, pixels_ref.shape[0] // unroll, some, 0)
+
+
+def transform_patch(matrix_ref, low, wide, high, out_ref):
+    transform(matrix_ref, low, out_ref, 0, low.shape[0])
+    transform(matrix_ref, wide, out_ref, RADIUS, 8)
+    transform(matrix_ref, high, out_ref, RADIUS + TILE, high.shape[0])
 
 
 def back(matrix_ref, spectrum_ref, row):
@@ -93,9 +98,9 @@
     lax.fori_loop(0, 2, lane_step, 0)
 
 
-def taps_kernel(left, centre, right, grad, patch_mat, tile_mat, inv_mat, out_ref, wide, tile, sums):
-    transform(patch_mat, [left, centre, right], wide, PATCH, 6)
-    transform(tile_mat, [grad], tile, TILE, 4)
+def taps_kernel(low, centre, high, grad, patch_mat, tile_mat, inv_mat, out_ref, wide, tile, sums):
+    transform(tile_mat, grad, tile, 0, 8)
+    transform_patch(patch_mat, low, centre, high, wide)
     block = 9
 
     def work(re, im):
@@ -124,9 +129,9 @@
     out_ref[KS * KS :, :] = jnp.zeros((out_ref.shape[0] - KS * KS, out_ref.shape[1]), jnp.float32)
 
 
-def conv_kernel(left, centre, right, taps, grad, patch_mat, taps_mat, inv_mat, out_ref, wide, filt, sums):
-    transform(patch_mat, [left, centre, right], wide, PATCH, 6)
-    transform(taps_mat, [taps], filt, KS, 3)
+def conv_kernel(low, centre, high, taps, grad, patch_mat, taps_mat, inv_mat, out_ref, wide, filt, sums):
+    transform(taps_mat, taps, filt, 0, 9)
+    transform_patch(patch_mat, low, centre, high, wide)
     block = 8
 
     def work(re, im):
@@ -202,10 +207,10 @@
 
 
 def halo(block):
-    low = shifted(block[-RADIUS:], ROW, 1)
-    high = shifted(block[:RADIUS], ROW, -1)
-    tall = jnp.concatenate([low, block, high], axis=0)
-    return (shifted(tall, COL, 1), tall, shifted(tall, COL, -1))
+    wide = jnp.concatenate([shifted(block, COL, 1), block, shifted(block, COL, -1)], axis=1)
+    low = shifted(wide[-RADIUS:], ROW, 1)
+    high = shifted(wide[:RADIUS], ROW, -1)
+    return (low, wide, high)
 
 
 def gelu_parts(values):
@@ -240,12 +245,16 @@
     return lax.all_to_all(copies, axes, 0, 0).reshape(count * block.shape[0], LANES)
 
 
-def summed(blocks, scale):
-    flat = jnp.concatenate([to_rows(block.astype(jnp.bfloat16)) for block in blocks], axis=0)
-    half = scatter_sum(flat, "core")
-    part = scatter_sum(half.astype(jnp.bfloat16), PLANE)
+def summed(dense, taps, scale):
+    halves = []
+    for blocks in (dense, [taps]):
+        flat = jnp.concatenate([to_rows(block.astype(jnp.bfloat16)) for block in blocks], axis=0)
+        halves.append(scatter_sum(flat, "core").astype(jnp.bfloat16))
+    part = scatter_sum(jnp.concatenate(halves, axis=0), PLANE)
     total = (scatter_sum(part, "z") * scale).astype(jnp.bfloat16)
-    return gathered(gathered(gathered(total, "z"), PLANE), "core")
+    both = gathered(gathered(gathered(total, "z"), PLANE), "core").reshape(2, -1, LANES)
+    split = halves[0].shape[0]
+    return both[:, :split].reshape(-1, LANES), both[:, split:].reshape(-1, LANES)
 
 
 def per_device(inputs, stored, upstream, weight_in, weight_out, kernel):
@@ -270,11 +279,11 @@
     grad_inputs = conv_backward(sides_mid, kernel, grad_mid)
     pixel_count = tile_rows * tile_cols * lax.axis_size(ROW) * lax.axis_size(COL)
     grad_scale = 1.0 / math.sqrt(pixel_count)
-    final = summed([sum_in, sum_out, tap_sums], grad_scale)
+    final_dense, final_taps = summed([sum_in, sum_out], tap_sums, grad_scale)
     rows_in = sum_in.size // LANES
-    final_in = from_rows(final[:rows_in], sum_in.shape)
-    final_out = from_rows(final[rows_in : 2 * rows_in], sum_out.shape)
-    final_kernel = from_rows(final[2 * rows_in :], tap_sums.shape)[: KS * KS].reshape(KS, KS, channels)
+    final_in = from_rows(final_dense[:rows_in], sum_in.shape)
+    final_out = from_rows(final_dense[rows_in:], sum_out.shape)
+    final_kernel = from_rows(final_taps, tap_sums.shape)[: KS * KS].reshape(KS, KS, channels)
     return (grad_inputs, final_in, final_out, final_kernel)
 
 

time: 132 us -> 135 us (1.023)
  waiting for transfers between devices: 21.3 us -> 14.8 us
  blocking collectives: 40.2 us -> 45.4 us
  starting transfers between devices: 44.5 us -> 49.2 us
  Pallas kernels: 12.4 us -> 10.5 us
    all_to_all x1, waiting for transfers between devices: 5.95 us -> 2.14 us  [scatter_sum(): arrived = lax.all_to_all(parts, axes, 0, 0)]
    all_to_all x1, blocking collectives: 7.03 us -> 10.2 us  [gathered(): lax.all_to_all(copies, axes, 0, 0).reshape(count * block.shape[0], LANES)]
    all_to_all x1, starting transfers between devices: 5.35 us -> 8.47 us  [scatter_sum(): arrived = lax.all_to_all(parts, axes, 0, 0)]
    all_to_all x2, waiting for transfers between devices: 11.1 us -> 8.16 us  [gathered(): lax.all_to_all(copies, axes, 0, 0).reshape(count * block.shape[0], LANES)]
    all_to_all x2 -> x3, blocking collectives: 33.1 us -> 35.1 us  [scatter_sum(): arrived = lax.all_to_all(parts, axes, 0, 0)]
    pallas_call x2, Pallas kernels: 12.4 us -> 10.5 us  [spectral_call(): pl.pallas_call(kernel, out_shape=out_shape, in_specs=[pl.BlockSpec(memory...]
  transfers between devices with their start and end apart: 11 -> 11, of which waited for: 5 -> 5; matrix products, arithmetic and copies ran while one was open for 4% -> 5% of each run, Pallas kernels for 5% -> 4%
where the time goes in v3:
time: 135 us; the launch traced here: 134 us
  starting transfers between devices  49.2 us (36%)
  blocking collectives  45.4 us (34%)
  waiting for transfers between devices  14.8 us (11%)
  Pallas kernels  10.5 us (8%)
  local copies, waits for them, and re-layouts  8.18 us (6%)
  matrix products  3.27 us (2%)
  other arithmetic  1.55 us (1%)
    all_to_all x3, blocking collectives, scatter_sum(): arrived = lax.all_to_all(parts, axes, 0, 0)  35.1 us
    ppermute x8, starting transfers between devices, shifted(): return lax.ppermute(block, axes, pairs)  27.7 us
    all_to_all x2, starting transfers between devices, gathered(): lax.all_to_all(copies, axes, 0, 0).reshape(count * block.shape[0], LANES)  13 us
    pallas_call x2, Pallas kernels, spectral_call(): pl.pallas_call(kernel, out_shape=out_shape, in_specs=[pl.BlockSpec(memory...  10.5 us
    all_to_all x1, blocking collectives, gathered(): lax.all_to_all(copies, axes, 0, 0).reshape(count * block.shape[0], LANES)  10.2 us
    all_to_all x1, starting transfers between devices, scatter_sum(): arrived = lax.all_to_all(parts, axes, 0, 0)  8.47 us
    all_to_all x2, waiting for transfers between devices, gathered(): lax.all_to_all(copies, axes, 0, 0).reshape(count * block.shape[0], LANES)  8.16 us
    ppermute x8, waiting for transfers between devices, shifted(): return lax.ppermute(block, axes, pairs)  4.52 us
  transfers between devices with their start and end apart: 11, of which 5 were waited for; matrix products, arithmetic and copies ran while one was open for 5% of the time, Pallas kernels for 4%

profile of v3, /device:TPU:1, one launch (start us, length us, event | category | flops | bytes accessed | tf_op | source)
XLA Modules:
  0.0 134.0 jit_solution(451593567612946535)
XLA Ops:
  0.6 0.0 copy-start
  0.6 0.0 copy-start.9
  0.7 5.2 %collective-permute-start.4 = (bf16[16,16,256]{2,1,0:T(8,128)(2,1)}, bf16[16,16,256]{2,1,0:T(8,128)(2,1)}, u32[]{:S(2)}, u32[]{:S(2)}) collective-permute-start(bf16[16,16,256]{2,1,0:T(8,128)(2,1)} %param.12), channel_id=1, source_target_pairs={{0,1},{1,2},{2,3},{3,4},{4,5},{5,6},{6,7},{7,8},{8,9},{9,10},{10,1... | collective-permute-start | bytes 393224 | tf_op jit(solution)/shard_map/ppermute | solution.py:206
  5.8 1.3 collective-permute-start.5
  7.1 0.0 copy-done
  7.1 1.2 fusion.19
  8.3 0.0 copy-done.9
  8.3 0.0 copy-start.11
  8.3 0.6 convolution_convert_fusion
  8.9 0.4 copy-done.11
  9.4 0.8 fusion
  10.2 0.1 copy-done.7
  10.3 0.4 fusion.1
  10.6 0.2 copy.18
  10.9 0.0 copy-start.10
  10.9 0.1 copy.22
  11.0 0.1 copy.19
  11.1 0.0 collective-permute-done.4
  11.1 0.9 constant_dynamic-update-slice_fusion.2
  12.0 0.0 copy-done.10
  12.0 0.0 collective-permute-done.5
  12.0 0.9 constant_dynamic-update-slice_fusion.centre
  13.0 0.9 fusion.17
  13.8 6.6 %collective-permute-start.7 = (bf16[13,48,256]{2,1,0:T(8,128)(2,1)}, bf16[13,48,256]{2,1,0:T(8,128)(2,1)S(1)}, u32[]{:S(2)}, u32[]{:S(2)}) collective-permute-start(bf16[13,48,256]{2,1,0:T(8,128)(2,1)} %get-tuple-element.6), channel_id=1, source_target_pairs={{32,0},{64,32},{96,64},{128,96},{160,128},{192,160},{224,192},{256... | collective-permute-start | bytes 958472 | tf_op jit(solution)/shard_map/ppermute | solution.py:206
  20.4 1.9 %collective-permute-start.6 = (bf16[13,48,256]{2,1,0:T(8,128)(2,1)}, bf16[13,48,256]{2,1,0:T(8,128)(2,1)S(1)}, u32[]{:S(2)}, u32[]{:S(2)}) collective-permute-start(bf16[13,48,256]{2,1,0:T(8,128)(2,1)} %get-tuple-element.7), channel_id=1, source_target_pairs={{0,32},{32,64},{64,96},{96,128},{128,160},{160,192},{192,224},{224... | collective-permute-start | bytes 958472 | tf_op jit(solution)/shard_map/ppermute | solution.py:206
  22.4 0.1 pad_maximum_fusion
  22.4 4.7 %all_to_all.35 = bf16[2,2048,128]{2,1,0:T(8,128)(2,1)S(1)} all-to-all(bf16[2,2048,128]{2,1,0:T(8,128)(2,1)S(1)} %bitcast.56), channel_id=1, replica_groups=mesh['yh'=2,'x'=4,'core'=2,'yl'=2,'z'=16] {'core'}, dimensions={0} | all-to-all | bytes 2097152 | tf_op jit(solution)/shard_map/all_to_all | solution.py:238
  27.2 1.1 reduce_sum.42
  28.3 0.3 fusion.2
  28.6 0.0 collective-permute-done.7.high
  28.6 0.0 collective-permute-done.6.low
  28.6 0.0 copy-done.1
  28.7 4.7 %shard_map.148 = f32[768,256]{1,0:T(8,128)S(1)} custom-call(bf16[13,48,256]{2,1,0:T(8,128)(2,1)S(1)} %collective-permute-done.6.low, bf16[16,48,256]{2,1,0:T(8,128)(2,1)S(1)} %constant_dynamic-update-slice_fusion.centre, bf16[13,48,256]{2,1,0:T(8,128)(2,1)S(1)} %collective-permute-done.7.high, bf16[16,16,256]{2,1,0:T(8,128)(2,1)S(1)} %bitcast.51, ...), custom_call_target="tpu_custom_call" | custom-call | flops 4000000000 | bytes 8000000 | tf_op jit(solution)/shard_map/pallas_call | solution.py:165
  33.3 0.0 copy-start.6
  33.4 4.2 %all_to_all.36 = bf16[2,768,128]{2,1,0:T(8,128)(2,1)S(1)} all-to-all(bf16[2,768,128]{2,1,0:T(8,128)(2,1)S(1)} %bitcast.62), channel_id=1, replica_groups=mesh['yh'=2,'x'=4,'core'=2,'yl'=2,'z'=16] {'core'}, dimensions={0} | all-to-all | bytes 786432 | tf_op jit(solution)/shard_map/all_to_all | solution.py:238
  37.6 0.1 reduce_sum.43
  37.8 26.2 %all_to_all.37 = bf16[16,176,128]{2,1,0:T(8,128)(2,1)S(1)} all-to-all(bf16[16,176,128]{2,1,0:T(8,128)(2,1)S(1)} %bitcast.58), channel_id=1, replica_groups=mesh['yh'=2,'x'=4,'core'=2,'yl'=2,'z'=16] {'x','yh','yl'}, dimensions={0} | all-to-all | bytes 1441792 | tf_op jit(solution)/shard_map/all_to_all | solution.py:238
  64.0 0.1 convert_reduce_fusion
  64.1 0.7 reshape.80
  64.8 8.5 %all-to-all-start.3 = ((f32[16,11,128]{2,1,0:T(8,128)}), f32[16,11,128]{2,1,0:T(8,128)S(1)}, u32[]{:S(2)}, u32[]{:S(2)}) async-start(f32[16,11,128]{2,1,0:T(8,128)} %reshape.80), calls=%async_computation.3 | async-start | bytes 262144 | tf_op jit(solution)/shard_map/all_to_all | solution.py:238
  73.3 1.3 collective-permute-start.1
  74.6 4.0 %collective-permute-start = (bf16[16,16,256]{2,1,0:T(8,128)(2,1)S(1)}, bf16[16,16,256]{2,1,0:T(8,128)(2,1)S(1)}, u32[]{:S(2)}, u32[]{:S(2)}) collective-permute-start(bf16[16,16,256]{2,1,0:T(8,128)(2,1)S(1)} %bitcast.53), channel_id=1, source_target_pairs={{0,1},{1,2},{2,3},{3,4},{4,5},{5,6},{6,7},{7,8},{8,9},{9,10},{10,1... | collective-permute-start | bytes 393224 | tf_op jit(solution)/shard_map/ppermute | solution.py:206
  78.6 4.4 %collective-permute-done.1 = bf16[16,16,256]{2,1,0:T(8,128)(2,1)S(1)} collective-permute-done((bf16[16,16,256]{2,1,0:T(8,128)(2,1)S(1)}, bf16[16,16,256]{2,1,0:T(8,128)(2,1)S(1)}, u32[]{:S(2)}, u32[]{:S(2)}) %collective-permute-start.1) | collective-permute-done | bytes 131104 | tf_op jit(solution)/shard_map/ppermute | solution.py:206
  83.0 0.1 collective-permute-done
  83.1 2.1 %all-to-all-done.3 = f32[16,11,128]{2,1,0:T(8,128)S(1)} async-done(((f32[16,11,128]{2,1,0:T(8,128)}), f32[16,11,128]{2,1,0:T(8,128)S(1)}, u32[]{:S(2)}, u32[]{:S(2)}) %all-to-all-start.3) | async-done | bytes 90144 | tf_op jit(solution)/shard_map/all_to_all | solution.py:238
  85.3 0.6 broadcast_in_dim.20
  85.9 9.2 %all-to-all-start.4 = ((bf16[16,11,128]{2,1,0:T(8,128)(2,1)}), bf16[16,11,128]{2,1,0:T(8,128)(2,1)S(1)}, u32[]{:S(2)}, u32[]{:S(2)}) async-start(bf16[16,11,128]{2,1,0:T(8,128)(2,1)} %broadcast_in_dim.20), calls=%async_computation.4 | async-start | bytes 131072 | tf_op jit(solution)/shard_map/all_to_all | solution.py:245
  95.2 0.0 copy-start.8
  95.2 5.6 %collective-permute-start.3 = (bf16[13,48,256]{2,1,0:T(8,128)(2,1)S(1)}, bf16[13,48,256]{2,1,0:T(8,128)(2,1)S(1)}, u32[]{:S(2)}, u32[]{:S(2)}) collective-permute-start(bf16[13,48,256]{2,1,0:T(8,128)(2,1)S(1)} %get-tuple-element.8), channel_id=1, source_target_pairs={{32,0},{64,32},{96,64},{128,96},{160,128},{192,160},{224,192},{256... | collective-permute-start | bytes 958472 | tf_op jit(solution)/shard_map/ppermute | solution.py:206
  100.8 1.9 %collective-permute-start.2 = (bf16[13,48,256]{2,1,0:T(8,128)(2,1)S(1)}, bf16[13,48,256]{2,1,0:T(8,128)(2,1)S(1)}, u32[]{:S(2)}, u32[]{:S(2)}) collective-permute-start(bf16[13,48,256]{2,1,0:T(8,128)(2,1)S(1)} %get-tuple-element.9), channel_id=1, source_target_pairs={{0,32},{32,64},{64,96},{96,128},{128,160},{160,192},{192,224},{224... | collective-permute-start | bytes 958472 | tf_op jit(solution)/shard_map/ppermute | solution.py:206
  102.7 4.0 %all-to-all-done.4 = bf16[16,11,128]{2,1,0:T(8,128)(2,1)S(1)} async-done(((bf16[16,11,128]{2,1,0:T(8,128)(2,1)}), bf16[16,11,128]{2,1,0:T(8,128)(2,1)S(1)}, u32[]{:S(2)}, u32[]{:S(2)}) %all-to-all-start.4) | async-done | bytes 45088 | tf_op jit(solution)/shard_map/all_to_all | solution.py:245
  106.8 0.0 copy-start.3
  106.8 0.0 copy-start.5
  106.8 1.0 broadcast_in_dim.22
  107.8 3.8 %all-to-all-start.5 = ((bf16[16,176,128]{2,1,0:T(8,128)(2,1)}), bf16[16,176,128]{2,1,0:T(8,128)(2,1)S(1)}, u32[]{:S(2)}, u32[]{:S(2)}) async-start(bf16[16,176,128]{2,1,0:T(8,128)(2,1)} %broadcast_in_dim.22), calls=%async_computation.5 | async-start | bytes 1441792 | tf_op jit(solution)/shard_map/all_to_all | solution.py:245
  111.6 0.0 copy-done.8
  111.6 0.0 collective-permute-done.3.high
  111.6 0.0 collective-permute-done.2.low
  111.7 5.8 %shard_map.147 = bf16[16,16,256]{2,1,0:T(8,128)(2,1)} custom-call(bf16[13,48,256]{2,1,0:T(8,128)(2,1)S(1)} %collective-permute-done.2.low, bf16[16,48,256]{2,1,0:T(8,128)(2,1)S(1)} %pad_maximum_fusion.2.centre, bf16[13,48,256]{2,1,0:T(8,128)(2,1)S(1)} %collective-permute-done.3.high, bf16[27,32,256]{2,1,0:T(8,128)(2,1)S(1)} %pad.4.taps, ...), custom_call_target="tpu_custom_call" | custom-call | flops 4000000000 | bytes 8000000 | tf_op jit(solution)/shard_map/pallas_call | solution.py:165
  117.5 4.2 %all-to-all-done.5 = bf16[16,176,128]{2,1,0:T(8,128)(2,1)S(1)} async-done(((bf16[16,176,128]{2,1,0:T(8,128)(2,1)}), bf16[16,176,128]{2,1,0:T(8,128)(2,1)S(1)}, u32[]{:S(2)}, u32[]{:S(2)}) %all-to-all-start.5) | async-done | bytes 720928 | tf_op jit(solution)/shard_map/all_to_all | solution.py:245
  121.7 0.1 broadcast_in_dim.24
  121.8 10.2 %all_to_all.38 = bf16[2,2816,128]{2,1,0:T(8,128)(2,1)S(1)} all-to-all(bf16[2,2816,128]{2,1,0:T(8,128)(2,1)S(1)} %broadcast_in_dim.24), channel_id=1, replica_groups=mesh['yh'=2,'x'=4,'core'=2,'yl'=2,'z'=16] {'core'}, dimensions={0} | all-to-all | bytes 2883584 | tf_op jit(solution)/shard_map/all_to_all | solution.py:245
  132.1 0.9 reshape.86
  132.9 1.0 fusion.16
  (20 shorter events, 0.3 us)
Async XLA Ops:
  0.6 6.5 %copy-start = (bf16[256,1024]{1,0:T(8,128)(2,1)S(1)}, bf16[256,1024]{1,0:T(8,128)(2,1)}, u32[]{:S(2)}) copy-start(bf16[256,1024]{1,0:T(8,128)(2,1)} %param.15) | copy-start | bytes 1572868
  0.6 7.7 %copy-start.9 = (bf16[16,16,256]{2,1,0:T(8,128)(2,1)S(1)}, bf16[16,16,256]{2,1,0:T(8,128)(2,1)}, u32[]{:S(2)}) copy-start(bf16[16,16,256]{2,1,0:T(8,128)(2,1)} %param.14) | copy-start | bytes 393220
  0.7 10.4 %collective-permute-start.4 = (bf16[16,16,256]{2,1,0:T(8,128)(2,1)}, bf16[16,16,256]{2,1,0:T(8,128)(2,1)}, u32[]{:S(2)}, u32[]{:S(2)}) collective-permute-start(bf16[16,16,256]{2,1,0:T(8,128)(2,1)} %param.12), channel_id=1, source_target_pairs={{0,1},{1,2},{2,3},{3,4},{4,5},{5,6},{6,7},{7,8},{8,9},{9,10},{10,1... | collective-permute-start | bytes 393224 | tf_op jit(solution)/shard_map/ppermute | solution.py:206
  5.8 6.2 %collective-permute-start.5 = (bf16[16,16,256]{2,1,0:T(8,128)(2,1)}, bf16[16,16,256]{2,1,0:T(8,128)(2,1)}, u32[]{:S(2)}, u32[]{:S(2)}) collective-permute-start(bf16[16,16,256]{2,1,0:T(8,128)(2,1)} %param.12), channel_id=1, source_target_pairs={{1,0},{2,1},{3,2},{4,3},{5,4},{6,5},{7,6},{8,7},{9,8},{10,9},{11,1... | collective-permute-start | bytes 393224 | tf_op jit(solution)/shard_map/ppermute | solution.py:206
  8.3 1.0 copy-start.11
  9.4 0.9 copy-start.7
  10.9 1.1 copy-start.10
  13.8 14.8 %collective-permute-start.7 = (bf16[13,48,256]{2,1,0:T(8,128)(2,1)}, bf16[13,48,256]{2,1,0:T(8,128)(2,1)S(1)}, u32[]{:S(2)}, u32[]{:S(2)}) collective-permute-start(bf16[13,48,256]{2,1,0:T(8,128)(2,1)} %get-tuple-element.6), channel_id=1, source_target_pairs={{32,0},{64,32},{96,64},{128,96},{160,128},{192,160},{224,192},{256... | collective-permute-start | bytes 958472 | tf_op jit(solution)/shard_map/ppermute | solution.py:206
  20.4 8.2 %collective-permute-start.6 = (bf16[13,48,256]{2,1,0:T(8,128)(2,1)}, bf16[13,48,256]{2,1,0:T(8,128)(2,1)S(1)}, u32[]{:S(2)}, u32[]{:S(2)}) collective-permute-start(bf16[13,48,256]{2,1,0:T(8,128)(2,1)} %get-tuple-element.7), channel_id=1, source_target_pairs={{0,32},{32,64},{64,96},{96,128},{128,160},{160,192},{192,224},{224... | collective-permute-start | bytes 958472 | tf_op jit(solution)/shard_map/ppermute | solution.py:206
  27.2 1.5 %copy-start.1 = (bf16[32,144]{1,0:T(8,128)(2,1)S(1)}, bf16[32,144]{1,0:T(8,128)(2,1)}, u32[]{:S(2)}) copy-start(bf16[32,144]{1,0:T(8,128)(2,1)} %constant.31.clone.inv_mat) | copy-start | bytes 27652
  27.2 1.5 %copy-start.2 = (bf16[48,96]{1,0:T(8,128)(2,1)S(1)}, bf16[48,96]{1,0:T(8,128)(2,1)}, u32[]{:S(2)}) copy-start(bf16[48,96]{1,0:T(8,128)(2,1)} %constant.29.clone.patch_mat) | copy-start | bytes 27652
  27.2 1.5 %copy-start.4 = (bf16[48,32]{1,0:T(8,128)(2,1)S(1)}, bf16[48,32]{1,0:T(8,128)(2,1)}, u32[]{:S(2)}) copy-start(bf16[48,32]{1,0:T(8,128)(2,1)} %constant.30.clone.tile_mat) | copy-start | bytes 9220
  33.3 4.4 %copy-start.6 = (bf16[2048,128]{1,0:T(8,128)(2,1)S(1)}, bf16[2048,128]{1,0:T(8,128)(2,1)}, u32[]{:S(2)}) copy-start(bf16[2048,128]{1,0:T(8,128)(2,1)} %reduce_sum.42) | copy-start | bytes 1572868
  64.8 20.5 %all-to-all-start.3 = ((f32[16,11,128]{2,1,0:T(8,128)}), f32[16,11,128]{2,1,0:T(8,128)S(1)}, u32[]{:S(2)}, u32[]{:S(2)}) async-start(f32[16,11,128]{2,1,0:T(8,128)} %reshape.80), calls=%async_computation.3 | async-start | bytes 262144 | tf_op jit(solution)/shard_map/all_to_all | solution.py:238
  73.3 9.7 %collective-permute-start.1 = (bf16[16,16,256]{2,1,0:T(8,128)(2,1)S(1)}, bf16[16,16,256]{2,1,0:T(8,128)(2,1)S(1)}, u32[]{:S(2)}, u32[]{:S(2)}) collective-permute-start(bf16[16,16,256]{2,1,0:T(8,128)(2,1)S(1)} %bitcast.52), channel_id=1, source_target_pairs={{1,0},{2,1},{3,2},{4,3},{5,4},{6,5},{7,6},{8,7},{9,8},{10,9},{11,1... | collective-permute-start | bytes 393224 | tf_op jit(solution)/shard_map/ppermute | solution.py:206
  74.6 8.5 %collective-permute-start = (bf16[16,16,256]{2,1,0:T(8,128)(2,1)S(1)}, bf16[16,16,256]{2,1,0:T(8,128)(2,1)S(1)}, u32[]{:S(2)}, u32[]{:S(2)}) collective-permute-start(bf16[16,16,256]{2,1,0:T(8,128)(2,1)S(1)} %bitcast.53), channel_id=1, source_target_pairs={{0,1},{1,2},{2,3},{3,4},{4,5},{5,6},{6,7},{7,8},{8,9},{9,10},{10,1... | collective-permute-start | bytes 393224 | tf_op jit(solution)/shard_map/ppermute | solution.py:206
  85.9 20.8 %all-to-all-start.4 = ((bf16[16,11,128]{2,1,0:T(8,128)(2,1)}), bf16[16,11,128]{2,1,0:T(8,128)(2,1)S(1)}, u32[]{:S(2)}, u32[]{:S(2)}) async-start(bf16[16,11,128]{2,1,0:T(8,128)(2,1)} %broadcast_in_dim.20), calls=%async_computation.4 | async-start | bytes 131072 | tf_op jit(solution)/shard_map/all_to_all | solution.py:245
  95.2 16.3 %copy-start.8 = (bf16[27,27,256]{2,1,0:T(8,128)(2,1)S(1)}, bf16[27,27,256]{2,1,0:T(8,128)(2,1)}, u32[]{:S(2)}) copy-start(bf16[27,27,256]{2,1,0:T(8,128)(2,1)} %param.17) | copy-start | bytes 1119748
  95.2 16.4 %collective-permute-start.3 = (bf16[13,48,256]{2,1,0:T(8,128)(2,1)S(1)}, bf16[13,48,256]{2,1,0:T(8,128)(2,1)S(1)}, u32[]{:S(2)}, u32[]{:S(2)}) collective-permute-start(bf16[13,48,256]{2,1,0:T(8,128)(2,1)S(1)} %get-tuple-element.8), channel_id=1, source_target_pairs={{32,0},{64,32},{96,64},{128,96},{160,128},{192,160},{224,192},{256... | collective-permute-start | bytes 958472 | tf_op jit(solution)/shard_map/ppermute | solution.py:206
  100.8 10.8 %collective-permute-start.2 = (bf16[13,48,256]{2,1,0:T(8,128)(2,1)S(1)}, bf16[13,48,256]{2,1,0:T(8,128)(2,1)S(1)}, u32[]{:S(2)}, u32[]{:S(2)}) collective-permute-start(bf16[13,48,256]{2,1,0:T(8,128)(2,1)S(1)} %get-tuple-element.9), channel_id=1, source_target_pairs={{0,32},{32,64},{64,96},{96,128},{128,160},{160,192},{192,224},{224... | collective-permute-start | bytes 958472 | tf_op jit(solution)/shard_map/ppermute | solution.py:206
  106.8 4.9 %copy-start.3 = (bf16[48,64]{1,0:T(8,128)(2,1)S(1)}, bf16[48,64]{1,0:T(8,128)(2,1)}, u32[]{:S(2)}) copy-start(bf16[48,64]{1,0:T(8,128)(2,1)} %constant.32.clone.taps_mat) | copy-start | bytes 18436
  106.8 4.9 %copy-start.5 = (bf16[16,144]{1,0:T(8,128)(2,1)S(1)}, bf16[16,144]{1,0:T(8,128)(2,1)}, u32[]{:S(2)}) copy-start(bf16[16,144]{1,0:T(8,128)(2,1)} %constant.33.clone.inv_mat) | copy-start | bytes 13828
  107.8 13.9 %all-to-all-start.5 = ((bf16[16,176,128]{2,1,0:T(8,128)(2,1)}), bf16[16,176,128]{2,1,0:T(8,128)(2,1)S(1)}, u32[]{:S(2)}, u32[]{:S(2)}) async-start(bf16[16,176,128]{2,1,0:T(8,128)(2,1)} %broadcast_in_dim.22), calls=%async_computation.5 | async-start | bytes 1441792 | tf_op jit(solution)/shard_map/all_to_all | solution.py:245

commit v4 on v3

--- a/solution.py
+++ b/solution.py
@@ -98,8 +98,8 @@
     lax.fori_loop(0, 2, lane_step, 0)
 
 
-def taps_kernel(low, centre, high, grad, patch_mat, tile_mat, inv_mat, out_ref, wide, tile, sums):
-    transform(tile_mat, grad, tile, 0, 8)
+def taps_kernel(low, centre, high, own, patch_mat, tile_mat, inv_mat, out_ref, wide, tile, sums):
+    transform(tile_mat, own, tile, 0, 8)
     transform_patch(patch_mat, low, centre, high, wide)
     block = 9
 
@@ -109,11 +109,12 @@
             real = [None] * block
             imag = [None] * block
             for i in range(TILE):
-                gr, gi = tile[i, re], tile[i, im]
+                xr, xi = tile[i, re], tile[i, im]
                 for a in range(block):
-                    xr, xi = wide[base + i + a, re], wide[base + i + a, im]
+                    row = i + KS - 1 - base - a
+                    gr, gi = wide[row, re], wide[row, im]
                     new_r = xr * gr + xi * gi
-                    new_i = xi * gr - xr * gi
+                    new_i = xr * gi - xi * gr
                     real[a] = new_r if i == 0 else real[a] + new_r
                     imag[a] = new_i if i == 0 else imag[a] + new_i
             for a in range(block):
@@ -177,14 +178,14 @@
     )(*args)
 
 
-def taps_gradient(sides, grad_tile):
+def taps_gradient(sides, own):
     mats = (
         forward_matrix(PATCH_POSITIONS),
         forward_matrix(list(range(TILE))),
-        inverse_matrix(range(KS), 32),
+        inverse_matrix(range(KS - 1, -1, -1), 32),
     )
-    args = (*sides, grad_tile, *(jnp.asarray(m) for m in mats))
-    out = jax.ShapeDtypeStruct((768, grad_tile.shape[-1]), jnp.float32)
+    args = (*sides, own, *(jnp.asarray(m) for m in mats))
+    out = jax.ShapeDtypeStruct((768, own.shape[-1]), jnp.float32)
     return spectral_call(taps_kernel, out, TILE, KS, args)
 
 
@@ -206,8 +207,22 @@
     return lax.ppermute(block, axes, pairs)
 
 
+def column_sides(block):
+    runs, depth = lax.axis_size("yl"), lax.axis_size("z")
+    ends = [(run * depth + depth - 1, (run + 1) * depth + depth - 1) for run in range(runs - 1)]
+    ends += [((run + 1) * depth, run * depth) for run in range(runs - 1)]
+    seam = lax.ppermute(block, COL, ends)
+    place = lax.axis_index("z")
+    up = jnp.where(place == depth - 1, seam, block)
+    down = jnp.where(place == 0, seam, block)
+    left = lax.ppermute(up, "z", [(i, (i + 1) % depth) for i in range(depth)])
+    right = lax.ppermute(down, "z", [(i, (i - 1) % depth) for i in range(depth)])
+    return left, right
+
+
 def halo(block):
-    wide = jnp.concatenate([shifted(block, COL, 1), block, shifted(block, COL, -1)], axis=1)
+    left, right = column_sides(block)
+    wide = jnp.concatenate([left, block, right], axis=1)
     low = shifted(wide[-RADIUS:], ROW, 1)
     high = shifted(wide[:RADIUS], ROW, -1)
     return (low, wide, high)
@@ -259,7 +274,6 @@
 
 def per_device(inputs, stored, upstream, weight_in, weight_out, kernel):
     tile_rows, tile_cols, channels = stored.shape
-    sides_in = halo(inputs)
     flat_z = stored.reshape(tile_rows * tile_cols, channels)
     flat_g = upstream.reshape(tile_rows * tile_cols, channels)
     hidden = jnp.dot(flat_z, weight_in, preferred_element_type=jnp.float32)
@@ -274,8 +288,8 @@
     sum_in = jnp.einsum("nc,nf->cf", flat_z, grad_hidden, preferred_element_type=jnp.float32)
     sum_out = jnp.einsum("nf,nc->fc", active, flat_g, preferred_element_type=jnp.float32)
     grad_mid = grad_flat.reshape(tile_rows, tile_cols, channels)
-    tap_sums = taps_gradient(sides_in, grad_mid)
     sides_mid = halo(grad_mid)
+    tap_sums = taps_gradient(sides_mid, inputs)
     grad_inputs = conv_backward(sides_mid, kernel, grad_mid)
     pixel_count = tile_rows * tile_cols * lax.axis_size(ROW) * lax.axis_size(COL)
     grad_scale = 1.0 / math.sqrt(pixel_count)

time: 135 us -> 130 us (0.963)
  blocking collectives: 45.4 us -> 72.9 us
  starting transfers between devices: 49.2 us -> 25.9 us
  waiting for transfers between devices: 14.8 us -> 9.19 us
  local copies, waits for them, and re-layouts: 8.18 us -> 5.47 us
    ppermute x8 -> x2, starting transfers between devices: 27.7 us -> 7.31 us  [shifted(): return lax.ppermute(block, axes, pairs)]
    all_to_all x1 -> x2, blocking collectives: 10.2 us -> 25.9 us  [gathered(): lax.all_to_all(copies, axes, 0, 0).reshape(count * block.shape[0], LANES)]
    ppermute x0 -> x3, starting transfers between devices: none -> 14.9 us  [the longest x1 11.6 us: column_sides(): lax.ppermute(down, 'z', [(i, (i - 1) % depth) for i in range(depth)])]
    all_to_all x3 -> x4, blocking collectives: 35.1 us -> 47 us  [scatter_sum(): arrived = lax.all_to_all(parts, axes, 0, 0)]
    all_to_all x2 -> x1, starting transfers between devices: 13 us -> 3.69 us  [gathered(): lax.all_to_all(copies, axes, 0, 0).reshape(count * block.shape[0], LANES)]
    all_to_all x1 -> x0, starting transfers between devices: 8.47 us -> none  [scatter_sum(): arrived = lax.all_to_all(parts, axes, 0, 0)]
    ppermute x0 -> x3, waiting for transfers between devices: none -> 4.98 us  [the longest x1 3.85 us: column_sides(): seam = lax.ppermute(block, COL, ends)]
    ppermute x8 -> x2, waiting for transfers between devices: 4.52 us -> 0.01 us  [shifted(): return lax.ppermute(block, axes, pairs)]
  transfers between devices with their start and end apart: 11 -> 6, of which waited for: 5 -> 3; matrix products, arithmetic and copies ran while one was open for 5% -> 2% of each run, Pallas kernels for 4% -> 5%
where the time goes in v4:
time: 130 us; the launch traced here: 129 us
  blocking collectives  72.9 us (56%)
  starting transfers between devices  25.9 us (20%)
  Pallas kernels  10.5 us (8%)
  waiting for transfers between devices  9.19 us (7%)
  local copies, waits for them, and re-layouts  5.47 us (4%)
  matrix products  3.26 us (3%)
    all_to_all x4, blocking collectives, scatter_sum(): arrived = lax.all_to_all(parts, axes, 0, 0)  47 us
    all_to_all x2, blocking collectives, gathered(): lax.all_to_all(copies, axes, 0, 0).reshape(count * block.shape[0], LANES)  25.9 us
    ppermute x1, starting transfers between devices, column_sides(): lax.ppermute(down, 'z', [(i, (i - 1) % depth) for i in range(depth)])  11.6 us
    pallas_call x2, Pallas kernels, spectral_call(): pl.pallas_call(kernel, out_shape=out_shape, in_specs=[pl.BlockSpec(memory...  10.5 us
    ppermute x2, starting transfers between devices, shifted(): return lax.ppermute(block, axes, pairs)  7.31 us
    all_to_all x1, waiting for transfers between devices, gathered(): lax.all_to_all(copies, axes, 0, 0).reshape(count * block.shape[0], LANES)  4.2 us
    ppermute x1, waiting for transfers between devices, column_sides(): seam = lax.ppermute(block, COL, ends)  3.85 us
    all_to_all x1, starting transfers between devices, gathered(): lax.all_to_all(copies, axes, 0, 0).reshape(count * block.shape[0], LANES)  3.69 us
  transfers between devices with their start and end apart: 6, of which 3 were waited for; matrix products, arithmetic and copies ran while one was open for 2% of the time, Pallas kernels for 5%

profile of v4, /device:TPU:1, one launch (start us, length us, event | category | flops | bytes accessed | tf_op | source)
XLA Modules:
  0.0 129.2 jit_solution(17071375442126587935)
XLA Ops:
  0.6 0.0 copy-start
  0.6 0.0 copy-start.10
  0.7 0.0 copy-start.9
  0.7 1.0 copy-done
  1.7 1.2 fusion.18
  2.9 0.0 copy-done.10
  2.9 0.0 copy-done.9
  2.9 0.8 fusion
  3.7 0.3 fusion.2
  4.0 0.0 copy-start.7
  4.1 1.4 %collective-permute-start = (bf16[16,16,256]{2,1,0:T(8,128)(2,1)S(1)}, bf16[16,16,256]{2,1,0:T(8,128)(2,1)S(1)}, u32[]{:S(2)}, u32[]{:S(2)}) collective-permute-start(bf16[16,16,256]{2,1,0:T(8,128)(2,1)S(1)} %bitcast.51), channel_id=1, source_target_pairs={{15,31},{16,0},{47,63},{48,32},{79,95},{80,64},{111,127},{112,96},... | collective-permute-start | bytes 393224 | tf_op jit(solution)/shard_map/ppermute | solution.py:214
  5.5 0.6 convolution_convert_fusion
  6.1 3.9 %collective-permute-done = bf16[16,16,256]{2,1,0:T(8,128)(2,1)S(1)} collective-permute-done((bf16[16,16,256]{2,1,0:T(8,128)(2,1)S(1)}, bf16[16,16,256]{2,1,0:T(8,128)(2,1)S(1)}, u32[]{:S(2)}, u32[]{:S(2)}) %collective-permute-start) | collective-permute-done | bytes 131104 | tf_op jit(solution)/shard_map/ppermute | solution.py:214
  10.0 1.9 %collective-permute-start.1 = (bf16[16,16,256]{2,1,0:T(8,128)(2,1)S(1)}, bf16[16,16,256]{2,1,0:T(8,128)(2,1)S(1)}, u32[]{:S(2)}, u32[]{:S(2)}) collective-permute-start(bf16[16,16,256]{2,1,0:T(8,128)(2,1)S(1)} %get-tuple-element.8), channel_id=1, source_target_pairs={{0,1},{1,2},{2,3},{3,4},{4,5},{5,6},{6,7},{7,8},{8,9},{9,10},{10,1... | collective-permute-start | bytes 393224 | tf_op jit(solution)/shard_map/ppermute | solution.py:218
  11.9 11.6 %collective-permute-start.2 = (bf16[16,16,256]{2,1,0:T(8,128)(2,1)S(1)}, bf16[16,16,256]{2,1,0:T(8,128)(2,1)S(1)}, u32[]{:S(2)}, u32[]{:S(2)}) collective-permute-start(bf16[16,16,256]{2,1,0:T(8,128)(2,1)S(1)} %get-tuple-element.9), channel_id=1, source_target_pairs={{0,15},{1,0},{2,1},{3,2},{4,3},{5,4},{6,5},{7,6},{8,7},{9,8},{10,9... | collective-permute-start | bytes 393224 | tf_op jit(solution)/shard_map/ppermute | solution.py:219
  23.4 0.0 copy-done.7
  23.5 0.4 fusion.1
  23.8 0.2 copy.18
  24.0 0.1 copy.22
  24.1 0.1 copy.19
  24.2 0.0 collective-permute-done.1
  24.2 1.1 collective-permute-done.2
  25.4 0.9 fusion.17
  26.3 4.3 %collective-permute-start.4 = (bf16[13,48,256]{2,1,0:T(8,128)(2,1)}, bf16[13,48,256]{2,1,0:T(8,128)(2,1)S(1)}, u32[]{:S(2)}, u32[]{:S(2)}) collective-permute-start(bf16[13,48,256]{2,1,0:T(8,128)(2,1)} %get-tuple-element.6), channel_id=1, source_target_pairs={{32,0},{64,32},{96,64},{128,96},{160,128},{192,160},{224,192},{256... | collective-permute-start | bytes 958472 | tf_op jit(solution)/shard_map/ppermute | solution.py:207
  30.6 3.0 %collective-permute-start.3 = (bf16[13,48,256]{2,1,0:T(8,128)(2,1)}, bf16[13,48,256]{2,1,0:T(8,128)(2,1)S(1)}, u32[]{:S(2)}, u32[]{:S(2)}) collective-permute-start(bf16[13,48,256]{2,1,0:T(8,128)(2,1)} %get-tuple-element.7), channel_id=1, source_target_pairs={{0,32},{32,64},{64,96},{96,128},{128,160},{160,192},{192,224},{224... | collective-permute-start | bytes 958472 | tf_op jit(solution)/shard_map/ppermute | solution.py:207
  33.6 0.1 pad_maximum_fusion
  33.7 0.0 copy-start.1
  33.7 0.0 copy-start.2
  33.7 0.0 copy-start.3
  33.7 0.0 copy-start.5
  33.7 4.3 %all_to_all.35 = bf16[2,2048,128]{2,1,0:T(8,128)(2,1)S(1)} all-to-all(bf16[2,2048,128]{2,1,0:T(8,128)(2,1)S(1)} %bitcast.55), channel_id=1, replica_groups=mesh['yh'=2,'x'=4,'core'=2,'yl'=2,'z'=16] {'core'}, dimensions={0} | all-to-all | bytes 2097152 | tf_op jit(solution)/shard_map/all_to_all | solution.py:253
  38.1 0.5 reduce_sum.42
  38.6 0.0 collective-permute-done.4.high
  38.6 0.0 collective-permute-done.3.low
  38.6 0.0 copy-done.1
  38.6 0.0 copy-done.2
  38.6 0.0 copy-done.3
  38.6 0.0 copy-done.5
  38.6 4.6 %shard_map.148 = f32[768,256]{1,0:T(8,128)S(1)} custom-call(bf16[13,48,256]{2,1,0:T(8,128)(2,1)S(1)} %collective-permute-done.3.low, bf16[16,48,256]{2,1,0:T(8,128)(2,1)S(1)} %pad_maximum_fusion.2.centre, bf16[13,48,256]{2,1,0:T(8,128)(2,1)S(1)} %collective-permute-done.4.high, bf16[16,16,256]{2,1,0:T(8,128)(2,1)S(1)} %copy-done.1, ...), custom_call_target="tpu_custom_call" | custom-call | flops 4000000000 | bytes 8000000 | tf_op jit(solution)/shard_map/pallas_call | solution.py:166
  43.3 4.1 %all_to_all.36 = bf16[2,768,128]{2,1,0:T(8,128)(2,1)S(1)} all-to-all(bf16[2,768,128]{2,1,0:T(8,128)(2,1)S(1)} %bitcast.61), channel_id=1, replica_groups=mesh['yh'=2,'x'=4,'core'=2,'yl'=2,'z'=16] {'core'}, dimensions={0} | all-to-all | bytes 786432 | tf_op jit(solution)/shard_map/all_to_all | solution.py:253
  47.4 0.1 reduce_sum.43
  47.6 22.2 %all_to_all.37 = bf16[16,176,128]{2,1,0:T(8,128)(2,1)S(1)} all-to-all(bf16[16,176,128]{2,1,0:T(8,128)(2,1)S(1)} %bitcast.57), channel_id=1, replica_groups=mesh['yh'=2,'x'=4,'core'=2,'yl'=2,'z'=16] {'x','yh','yl'}, dimensions={0} | all-to-all | bytes 1441792 | tf_op jit(solution)/shard_map/all_to_all | solution.py:253
  69.7 0.1 convert_reduce_fusion
  69.9 0.0 copy-start.8
  69.9 16.4 %all_to_all.38 = f32[16,11,128]{2,1,0:T(8,128)S(1)} all-to-all(f32[16,11,128]{2,1,0:T(8,128)S(1)} %reshape.80), channel_id=1, replica_groups=mesh['yh'=2,'x'=4,'core'=2,'yl'=2,'z'=16] {'z'}, dimensions={0} | all-to-all | bytes 180224 | tf_op jit(solution)/shard_map/all_to_all | solution.py:253
  86.3 16.8 %all_to_all.39 = bf16[16,11,128]{2,1,0:T(8,128)(2,1)S(1)} all-to-all(bf16[16,11,128]{2,1,0:T(8,128)(2,1)S(1)} %broadcast_in_dim.20), channel_id=1, replica_groups=mesh['yh'=2,'x'=4,'core'=2,'yl'=2,'z'=16] {'z'}, dimensions={0} | all-to-all | bytes 90112 | tf_op jit(solution)/shard_map/all_to_all | solution.py:260
  103.1 0.0 copy-start.4
  103.1 0.0 copy-start.6
  103.1 1.0 broadcast_in_dim.22
  104.1 3.7 %all-to-all-start.5 = ((bf16[16,176,128]{2,1,0:T(8,128)(2,1)}), bf16[16,176,128]{2,1,0:T(8,128)(2,1)S(1)}, u32[]{:S(2)}, u32[]{:S(2)}) async-start(bf16[16,176,128]{2,1,0:T(8,128)(2,1)} %broadcast_in_dim.22), calls=%async_computation.5 | async-start | bytes 1441792 | tf_op jit(solution)/shard_map/all_to_all | solution.py:260
  107.8 0.0 copy-done.8
  107.8 0.0 copy-done.4
  107.8 0.0 copy-done.6
  107.9 5.8 %shard_map.147 = bf16[16,16,256]{2,1,0:T(8,128)(2,1)} custom-call(bf16[13,48,256]{2,1,0:T(8,128)(2,1)S(1)} %collective-permute-done.3.low, bf16[16,48,256]{2,1,0:T(8,128)(2,1)S(1)} %pad_maximum_fusion.2.centre, bf16[13,48,256]{2,1,0:T(8,128)(2,1)S(1)} %collective-permute-done.4.high, bf16[27,32,256]{2,1,0:T(8,128)(2,1)S(1)} %pad.4.taps, ...), custom_call_target="tpu_custom_call" | custom-call | flops 4000000000 | bytes 8000000 | tf_op jit(solution)/shard_map/pallas_call | solution.py:166
  113.7 4.2 %all-to-all-done.5 = bf16[16,176,128]{2,1,0:T(8,128)(2,1)S(1)} async-done(((bf16[16,176,128]{2,1,0:T(8,128)(2,1)}), bf16[16,176,128]{2,1,0:T(8,128)(2,1)S(1)}, u32[]{:S(2)}, u32[]{:S(2)}) %all-to-all-start.5) | async-done | bytes 720928 | tf_op jit(solution)/shard_map/all_to_all | solution.py:260
  117.9 0.1 broadcast_in_dim.24
  118.0 9.2 %all_to_all.40 = bf16[2,2816,128]{2,1,0:T(8,128)(2,1)S(1)} all-to-all(bf16[2,2816,128]{2,1,0:T(8,128)(2,1)S(1)} %broadcast_in_dim.24), channel_id=1, replica_groups=mesh['yh'=2,'x'=4,'core'=2,'yl'=2,'z'=16] {'core'}, dimensions={0} | all-to-all | bytes 2883584 | tf_op jit(solution)/shard_map/all_to_all | solution.py:260
  127.2 0.9 reshape.86
  128.1 1.0 fusion.16
  (12 shorter events, 0.3 us)
Async XLA Ops:
  0.6 1.0 copy-start
  0.6 2.2 %copy-start.10 = (bf16[1024,256]{1,0:T(8,128)(2,1)S(1)}, bf16[1024,256]{1,0:T(8,128)(2,1)}, u32[]{:S(2)}) copy-start(bf16[1024,256]{1,0:T(8,128)(2,1)} %param.16) | copy-start | bytes 1572868
  0.7 2.2 %copy-start.9 = (bf16[16,16,256]{2,1,0:T(8,128)(2,1)S(1)}, bf16[16,16,256]{2,1,0:T(8,128)(2,1)}, u32[]{:S(2)}) copy-start(bf16[16,16,256]{2,1,0:T(8,128)(2,1)} %param.14) | copy-start | bytes 393220
  4.0 19.4 %copy-start.7 = (bf16[16,16,256]{2,1,0:T(8,128)(2,1)S(1)}, bf16[16,16,256]{2,1,0:T(8,128)(2,1)}, u32[]{:S(2)}) copy-start(bf16[16,16,256]{2,1,0:T(8,128)(2,1)} %param.13) | copy-start | bytes 393220
  4.1 5.9 %collective-permute-start = (bf16[16,16,256]{2,1,0:T(8,128)(2,1)S(1)}, bf16[16,16,256]{2,1,0:T(8,128)(2,1)S(1)}, u32[]{:S(2)}, u32[]{:S(2)}) collective-permute-start(bf16[16,16,256]{2,1,0:T(8,128)(2,1)S(1)} %bitcast.51), channel_id=1, source_target_pairs={{15,31},{16,0},{47,63},{48,32},{79,95},{80,64},{111,127},{112,96},... | collective-permute-start | bytes 393224 | tf_op jit(solution)/shard_map/ppermute | solution.py:214
  10.0 14.3 %collective-permute-start.1 = (bf16[16,16,256]{2,1,0:T(8,128)(2,1)S(1)}, bf16[16,16,256]{2,1,0:T(8,128)(2,1)S(1)}, u32[]{:S(2)}, u32[]{:S(2)}) collective-permute-start(bf16[16,16,256]{2,1,0:T(8,128)(2,1)S(1)} %get-tuple-element.8), channel_id=1, source_target_pairs={{0,1},{1,2},{2,3},{3,4},{4,5},{5,6},{6,7},{7,8},{8,9},{9,10},{10,1... | collective-permute-start | bytes 393224 | tf_op jit(solution)/shard_map/ppermute | solution.py:218
  11.9 13.5 %collective-permute-start.2 = (bf16[16,16,256]{2,1,0:T(8,128)(2,1)S(1)}, bf16[16,16,256]{2,1,0:T(8,128)(2,1)S(1)}, u32[]{:S(2)}, u32[]{:S(2)}) collective-permute-start(bf16[16,16,256]{2,1,0:T(8,128)(2,1)S(1)} %get-tuple-element.9), channel_id=1, source_target_pairs={{0,15},{1,0},{2,1},{3,2},{4,3},{5,4},{6,5},{7,6},{8,7},{9,8},{10,9... | collective-permute-start | bytes 393224 | tf_op jit(solution)/shard_map/ppermute | solution.py:219
  26.3 12.3 %collective-permute-start.4 = (bf16[13,48,256]{2,1,0:T(8,128)(2,1)}, bf16[13,48,256]{2,1,0:T(8,128)(2,1)S(1)}, u32[]{:S(2)}, u32[]{:S(2)}) collective-permute-start(bf16[13,48,256]{2,1,0:T(8,128)(2,1)} %get-tuple-element.6), channel_id=1, source_target_pairs={{32,0},{64,32},{96,64},{128,96},{160,128},{192,160},{224,192},{256... | collective-permute-start | bytes 958472 | tf_op jit(solution)/shard_map/ppermute | solution.py:207
  30.6 8.0 %collective-permute-start.3 = (bf16[13,48,256]{2,1,0:T(8,128)(2,1)}, bf16[13,48,256]{2,1,0:T(8,128)(2,1)S(1)}, u32[]{:S(2)}, u32[]{:S(2)}) collective-permute-start(bf16[13,48,256]{2,1,0:T(8,128)(2,1)} %get-tuple-element.7), channel_id=1, source_target_pairs={{0,32},{32,64},{64,96},{96,128},{128,160},{160,192},{192,224},{224... | collective-permute-start | bytes 958472 | tf_op jit(solution)/shard_map/ppermute | solution.py:207
  33.7 4.9 %copy-start.1 = (bf16[16,16,256]{2,1,0:T(8,128)(2,1)S(1)}, bf16[16,16,256]{2,1,0:T(8,128)(2,1)}, u32[]{:S(2)}) copy-start(bf16[16,16,256]{2,1,0:T(8,128)(2,1)} %own.1) | copy-start | bytes 393220
  33.7 4.9 %copy-start.2 = (bf16[32,144]{1,0:T(8,128)(2,1)S(1)}, bf16[32,144]{1,0:T(8,128)(2,1)}, u32[]{:S(2)}) copy-start(bf16[32,144]{1,0:T(8,128)(2,1)} %constant.38.clone.inv_mat) | copy-start | bytes 27652
  33.7 4.9 %copy-start.3 = (bf16[48,96]{1,0:T(8,128)(2,1)S(1)}, bf16[48,96]{1,0:T(8,128)(2,1)}, u32[]{:S(2)}) copy-start(bf16[48,96]{1,0:T(8,128)(2,1)} %constant.36.clone.patch_mat) | copy-start | bytes 27652
  33.7 4.9 %copy-start.5 = (bf16[48,32]{1,0:T(8,128)(2,1)S(1)}, bf16[48,32]{1,0:T(8,128)(2,1)}, u32[]{:S(2)}) copy-start(bf16[48,32]{1,0:T(8,128)(2,1)} %constant.37.clone.tile_mat) | copy-start | bytes 9220
  69.9 37.9 %copy-start.8 = (bf16[27,27,256]{2,1,0:T(8,128)(2,1)S(1)}, bf16[27,27,256]{2,1,0:T(8,128)(2,1)}, u32[]{:S(2)}) copy-start(bf16[27,27,256]{2,1,0:T(8,128)(2,1)} %param.17) | copy-start | bytes 1119748
  103.1 4.7 %copy-start.4 = (bf16[48,64]{1,0:T(8,128)(2,1)S(1)}, bf16[48,64]{1,0:T(8,128)(2,1)}, u32[]{:S(2)}) copy-start(bf16[48,64]{1,0:T(8,128)(2,1)} %constant.39.clone.taps_mat) | copy-start | bytes 18436
  103.1 4.7 %copy-start.6 = (bf16[16,144]{1,0:T(8,128)(2,1)S(1)}, bf16[16,144]{1,0:T(8,128)(2,1)}, u32[]{:S(2)}) copy-start(bf16[16,144]{1,0:T(8,128)(2,1)} %constant.40.clone.inv_mat) | copy-start | bytes 13828
  104.1 13.8 %all-to-all-start.5 = ((bf16[16,176,128]{2,1,0:T(8,128)(2,1)}), bf16[16,176,128]{2,1,0:T(8,128)(2,1)S(1)}, u32[]{:S(2)}, u32[]{:S(2)}) async-start(bf16[16,176,128]{2,1,0:T(8,128)(2,1)} %broadcast_in_dim.22), calls=%async_computation.5 | async-start | bytes 1441792 | tf_op jit(solution)/shard_map/all_to_all | solution.py:260

commit v5 on v4

--- a/solution.py
+++ b/solution.py
@@ -7,6 +7,7 @@
 from jax.experimental import pallas as pl
 from jax.experimental.pallas import tpu as pltpu
 from jax.sharding import Mesh, PartitionSpec as P
+
 
 KS = 27
 RADIUS = KS // 2
@@ -162,7 +163,6 @@
 
 
 def spectral_call(kernel, out_shape, second_rows, sum_rows, args):
-    channels = args[0].shape[-1]
     return pl.pallas_call(
         kernel,
         out_shape=out_shape,
@@ -207,21 +207,8 @@
     return lax.ppermute(block, axes, pairs)
 
 
-def column_sides(block):
-    runs, depth = lax.axis_size("yl"), lax.axis_size("z")
-    ends = [(run * depth + depth - 1, (run + 1) * depth + depth - 1) for run in range(runs - 1)]
-    ends += [((run + 1) * depth, run * depth) for run in range(runs - 1)]
-    seam = lax.ppermute(block, COL, ends)
-    place = lax.axis_index("z")
-    up = jnp.where(place == depth - 1, seam, block)
-    down = jnp.where(place == 0, seam, block)
-    left = lax.ppermute(up, "z", [(i, (i + 1) % depth) for i in range(depth)])
-    right = lax.ppermute(down, "z", [(i, (i - 1) % depth) for i in range(depth)])
-    return left, right
-
-
 def halo(block):
-    left, right = column_sides(block)
+    left, right = shifted(block, COL, 1), shifted(block, COL, -1)
     wide = jnp.concatenate([left, block, right], axis=1)
     low = shifted(wide[-RADIUS:], ROW, 1)
     high = shifted(wide[:RADIUS], ROW, -1)
@@ -272,7 +259,7 @@
     return both[:, :split].reshape(-1, LANES), both[:, split:].reshape(-1, LANES)
 
 
-def per_device(inputs, stored, upstream, weight_in, weight_out, kernel):
+def block_backward(inputs, stored, upstream, weight_in, weight_out, kernel):
     tile_rows, tile_cols, channels = stored.shape
     flat_z = stored.reshape(tile_rows * tile_cols, channels)
     flat_g = upstream.reshape(tile_rows * tile_cols, channels)
@@ -304,7 +291,7 @@
 def solution(mesh):
     fine = Mesh(mesh.devices.reshape(2, 4, 2, 2, 16), ("yh", "x", "core", "yl", "z"))
     return jax.shard_map(
-        per_device,
+        block_backward,
         mesh=fine,
         in_specs=(P(ROW, COL, None), P(ROW, COL, None), P(ROW, COL, None), P(), P(), P()),
         out_specs=(P(ROW, COL, None), P(), P(), P()),

time: 130 us -> 128 us (0.985)
  blocking collectives: 72.9 us -> 80.9 us
  starting transfers between devices: 25.9 us -> 20.9 us
  waiting for transfers between devices: 9.19 us -> 4.75 us
    ppermute x3 -> x0, starting transfers between devices: 14.9 us -> none  [the longest x1 11.6 us: column_sides(): lax.ppermute(down, 'z', [(i, (i - 1) % depth) for i in range(depth)])]
    ppermute x2 -> x4, starting transfers between devices: 7.31 us -> 17.2 us  [shifted(): return lax.ppermute(block, axes, pairs)]
    all_to_all x4, blocking collectives: 47 us -> 54.9 us  [scatter_sum(): arrived = lax.all_to_all(parts, axes, 0, 0)]
    ppermute x3 -> x0, waiting for transfers between devices: 4.98 us -> none  [the longest x1 3.85 us: column_sides(): seam = lax.ppermute(block, COL, ends)]
  transfers between devices with their start and end apart: 6 -> 5, of which waited for: 3 -> 2; matrix products, arithmetic and copies ran while one was open for 2% -> 2% of each run, Pallas kernels for 5% -> 5%
where the time goes in v5:
time: 128 us
  blocking collectives  80.9 us (63%)
  starting transfers between devices  20.9 us (16%)
  Pallas kernels  10.5 us (8%)
  local copies, waits for them, and re-layouts  5.46 us (4%)
  waiting for transfers between devices  4.75 us (4%)
  matrix products  3.26 us (3%)
    all_to_all x4, blocking collectives, scatter_sum(): arrived = lax.all_to_all(parts, axes, 0, 0)  54.9 us
    all_to_all x2, blocking collectives, gathered(): lax.all_to_all(copies, axes, 0, 0).reshape(count * block.shape[0], LANES)  25.9 us
    ppermute x4, starting transfers between devices, shifted(): return lax.ppermute(block, axes, pairs)  17.2 us
    pallas_call x2, Pallas kernels, spectral_call(): pl.pallas_call(kernel, out_shape=out_shape, in_specs=[pl.BlockSpec(memory...  10.5 us
    all_to_all x1, waiting for transfers between devices, gathered(): lax.all_to_all(copies, axes, 0, 0).reshape(count * block.shape[0], LANES)  4.21 us
    all_to_all x1, starting transfers between devices, gathered(): lax.all_to_all(copies, axes, 0, 0).reshape(count * block.shape[0], LANES)  3.69 us
  transfers between devices with their start and end apart: 5, of which 2 were waited for; matrix products, arithmetic and copies ran while one was open for 2% of the time, Pallas kernels for 5%

profile of v5, /device:TPU:1, one launch (start us, length us, event | category | flops | bytes accessed | tf_op | source)
XLA Modules:
  0.0 127.6 jit_solution(5763612382066393465)
XLA Ops:
  0.6 0.0 copy-start
  0.6 0.0 copy-start.10
  0.7 0.0 copy-start.9
  0.7 1.0 copy-done
  1.7 1.2 fusion.18
  2.9 0.0 copy-done.10
  2.9 0.0 copy-done.9
  2.9 0.8 fusion
  3.7 0.3 fusion.2
  4.0 0.0 copy-start.7
  4.1 1.4 %collective-permute-start.1 = (bf16[16,16,256]{2,1,0:T(8,128)(2,1)S(1)}, bf16[16,16,256]{2,1,0:T(8,128)(2,1)S(1)}, u32[]{:S(2)}, u32[]{:S(2)}) collective-permute-start(bf16[16,16,256]{2,1,0:T(8,128)(2,1)S(1)} %bitcast.51), channel_id=1, source_target_pairs={{1,0},{2,1},{3,2},{4,3},{5,4},{6,5},{7,6},{8,7},{9,8},{10,9},{11,1... | collective-permute-start | bytes 393224 | tf_op jit(solution)/shard_map/ppermute | solution.py:207
  5.5 5.0 %collective-permute-start = (bf16[16,16,256]{2,1,0:T(8,128)(2,1)S(1)}, bf16[16,16,256]{2,1,0:T(8,128)(2,1)S(1)}, u32[]{:S(2)}, u32[]{:S(2)}) collective-permute-start(bf16[16,16,256]{2,1,0:T(8,128)(2,1)S(1)} %bitcast.52), channel_id=1, source_target_pairs={{0,1},{1,2},{2,3},{3,4},{4,5},{5,6},{6,7},{7,8},{8,9},{9,10},{10,1... | collective-permute-start | bytes 393224 | tf_op jit(solution)/shard_map/ppermute | solution.py:207
  10.5 0.6 convolution_convert_fusion
  11.1 0.0 copy-done.7
  11.1 0.4 fusion.1
  11.5 0.2 copy.18
  11.7 0.1 copy.22
  11.8 0.1 copy.19
  11.9 0.0 collective-permute-done.1
  11.9 0.5 collective-permute-done
  12.4 0.9 fusion.17
  13.3 8.9 %collective-permute-start.3 = (bf16[13,48,256]{2,1,0:T(8,128)(2,1)}, bf16[13,48,256]{2,1,0:T(8,128)(2,1)S(1)}, u32[]{:S(2)}, u32[]{:S(2)}) collective-permute-start(bf16[13,48,256]{2,1,0:T(8,128)(2,1)} %get-tuple-element.6), channel_id=1, source_target_pairs={{32,0},{64,32},{96,64},{128,96},{160,128},{192,160},{224,192},{256... | collective-permute-start | bytes 958472 | tf_op jit(solution)/shard_map/ppermute | solution.py:207
  22.2 1.9 %collective-permute-start.2 = (bf16[13,48,256]{2,1,0:T(8,128)(2,1)}, bf16[13,48,256]{2,1,0:T(8,128)(2,1)S(1)}, u32[]{:S(2)}, u32[]{:S(2)}) collective-permute-start(bf16[13,48,256]{2,1,0:T(8,128)(2,1)} %get-tuple-element.7), channel_id=1, source_target_pairs={{0,32},{32,64},{64,96},{96,128},{128,160},{160,192},{192,224},{224... | collective-permute-start | bytes 958472 | tf_op jit(solution)/shard_map/ppermute | solution.py:207
  24.1 0.1 pad_maximum_fusion
  24.2 0.0 copy-start.1
  24.2 0.0 copy-start.2
  24.2 0.0 copy-start.3
  24.2 0.0 copy-start.5
  24.2 4.8 %all_to_all.35 = bf16[2,2048,128]{2,1,0:T(8,128)(2,1)S(1)} all-to-all(bf16[2,2048,128]{2,1,0:T(8,128)(2,1)S(1)} %bitcast.55), channel_id=1, replica_groups=mesh['yh'=2,'x'=4,'core'=2,'yl'=2,'z'=16] {'core'}, dimensions={0} | all-to-all | bytes 2097152 | tf_op jit(solution)/shard_map/all_to_all | solution.py:240
  29.1 0.5 reduce_sum.42
  29.6 0.0 collective-permute-done.3.high
  29.6 0.0 collective-permute-done.2.low
  29.6 0.0 copy-done.1
  29.6 0.0 copy-done.2
  29.6 0.0 copy-done.3
  29.7 0.0 copy-done.5
  29.7 4.6 %shard_map.148 = f32[768,256]{1,0:T(8,128)S(1)} custom-call(bf16[13,48,256]{2,1,0:T(8,128)(2,1)S(1)} %collective-permute-done.2.low, bf16[16,48,256]{2,1,0:T(8,128)(2,1)S(1)} %pad_maximum_fusion.2.centre, bf16[13,48,256]{2,1,0:T(8,128)(2,1)S(1)} %collective-permute-done.3.high, bf16[16,16,256]{2,1,0:T(8,128)(2,1)S(1)} %copy-done.1, ...), custom_call_target="tpu_custom_call" | custom-call | flops 4000000000 | bytes 8000000 | tf_op jit(solution)/shard_map/pallas_call | solution.py:166
  34.3 4.1 %all_to_all.36 = bf16[2,768,128]{2,1,0:T(8,128)(2,1)S(1)} all-to-all(bf16[2,768,128]{2,1,0:T(8,128)(2,1)S(1)} %bitcast.61), channel_id=1, replica_groups=mesh['yh'=2,'x'=4,'core'=2,'yl'=2,'z'=16] {'core'}, dimensions={0} | all-to-all | bytes 786432 | tf_op jit(solution)/shard_map/all_to_all | solution.py:240
  38.4 0.1 reduce_sum.43
  38.6 28.7 %all_to_all.37 = bf16[16,176,128]{2,1,0:T(8,128)(2,1)S(1)} all-to-all(bf16[16,176,128]{2,1,0:T(8,128)(2,1)S(1)} %bitcast.57), channel_id=1, replica_groups=mesh['yh'=2,'x'=4,'core'=2,'yl'=2,'z'=16] {'x','yh','yl'}, dimensions={0} | all-to-all | bytes 1441792 | tf_op jit(solution)/shard_map/all_to_all | solution.py:240
  67.3 0.1 convert_reduce_fusion
  67.4 0.0 copy-start.8
  67.4 17.3 %all_to_all.38 = f32[16,11,128]{2,1,0:T(8,128)S(1)} all-to-all(f32[16,11,128]{2,1,0:T(8,128)S(1)} %reshape.80), channel_id=1, replica_groups=mesh['yh'=2,'x'=4,'core'=2,'yl'=2,'z'=16] {'z'}, dimensions={0} | all-to-all | bytes 180224 | tf_op jit(solution)/shard_map/all_to_all | solution.py:240
  84.8 16.8 %all_to_all.39 = bf16[16,11,128]{2,1,0:T(8,128)(2,1)S(1)} all-to-all(bf16[16,11,128]{2,1,0:T(8,128)(2,1)S(1)} %broadcast_in_dim.20), channel_id=1, replica_groups=mesh['yh'=2,'x'=4,'core'=2,'yl'=2,'z'=16] {'z'}, dimensions={0} | all-to-all | bytes 90112 | tf_op jit(solution)/shard_map/all_to_all | solution.py:247
  101.6 0.0 copy-start.4
  101.6 0.0 copy-start.6
  101.6 1.0 broadcast_in_dim.22
  102.6 3.7 %all-to-all-start.5 = ((bf16[16,176,128]{2,1,0:T(8,128)(2,1)}), bf16[16,176,128]{2,1,0:T(8,128)(2,1)S(1)}, u32[]{:S(2)}, u32[]{:S(2)}) async-start(bf16[16,176,128]{2,1,0:T(8,128)(2,1)} %broadcast_in_dim.22), calls=%async_computation.5 | async-start | bytes 1441792 | tf_op jit(solution)/shard_map/all_to_all | solution.py:247
  106.3 0.0 copy-done.8
  106.3 0.0 copy-done.4
  106.3 0.0 copy-done.6
  106.3 5.8 %shard_map.147 = bf16[16,16,256]{2,1,0:T(8,128)(2,1)} custom-call(bf16[13,48,256]{2,1,0:T(8,128)(2,1)S(1)} %collective-permute-done.2.low, bf16[16,48,256]{2,1,0:T(8,128)(2,1)S(1)} %pad_maximum_fusion.2.centre, bf16[13,48,256]{2,1,0:T(8,128)(2,1)S(1)} %collective-permute-done.3.high, bf16[27,32,256]{2,1,0:T(8,128)(2,1)S(1)} %pad.4.taps, ...), custom_call_target="tpu_custom_call" | custom-call | flops 4000000000 | bytes 8000000 | tf_op jit(solution)/shard_map/pallas_call | solution.py:166
  112.2 4.2 %all-to-all-done.5 = bf16[16,176,128]{2,1,0:T(8,128)(2,1)S(1)} async-done(((bf16[16,176,128]{2,1,0:T(8,128)(2,1)}), bf16[16,176,128]{2,1,0:T(8,128)(2,1)S(1)}, u32[]{:S(2)}, u32[]{:S(2)}) %all-to-all-start.5) | async-done | bytes 720928 | tf_op jit(solution)/shard_map/all_to_all | solution.py:247
  116.4 0.1 broadcast_in_dim.24
  116.5 9.2 %all_to_all.40 = bf16[2,2816,128]{2,1,0:T(8,128)(2,1)S(1)} all-to-all(bf16[2,2816,128]{2,1,0:T(8,128)(2,1)S(1)} %broadcast_in_dim.24), channel_id=1, replica_groups=mesh['yh'=2,'x'=4,'core'=2,'yl'=2,'z'=16] {'core'}, dimensions={0} | all-to-all | bytes 2883584 | tf_op jit(solution)/shard_map/all_to_all | solution.py:247
  125.7 0.9 reshape.86
  126.6 1.0 fusion.16
  (11 shorter events, 0.3 us)
Async XLA Ops:
  0.6 1.0 copy-start
  0.6 2.2 %copy-start.10 = (bf16[1024,256]{1,0:T(8,128)(2,1)S(1)}, bf16[1024,256]{1,0:T(8,128)(2,1)}, u32[]{:S(2)}) copy-start(bf16[1024,256]{1,0:T(8,128)(2,1)} %param.16) | copy-start | bytes 1572868
  0.7 2.2 %copy-start.9 = (bf16[16,16,256]{2,1,0:T(8,128)(2,1)S(1)}, bf16[16,16,256]{2,1,0:T(8,128)(2,1)}, u32[]{:S(2)}) copy-start(bf16[16,16,256]{2,1,0:T(8,128)(2,1)} %param.14) | copy-start | bytes 393220
  4.0 7.0 %copy-start.7 = (bf16[16,16,256]{2,1,0:T(8,128)(2,1)S(1)}, bf16[16,16,256]{2,1,0:T(8,128)(2,1)}, u32[]{:S(2)}) copy-start(bf16[16,16,256]{2,1,0:T(8,128)(2,1)} %param.13) | copy-start | bytes 393220
  4.1 7.8 %collective-permute-start.1 = (bf16[16,16,256]{2,1,0:T(8,128)(2,1)S(1)}, bf16[16,16,256]{2,1,0:T(8,128)(2,1)S(1)}, u32[]{:S(2)}, u32[]{:S(2)}) collective-permute-start(bf16[16,16,256]{2,1,0:T(8,128)(2,1)S(1)} %bitcast.51), channel_id=1, source_target_pairs={{1,0},{2,1},{3,2},{4,3},{5,4},{6,5},{7,6},{8,7},{9,8},{10,9},{11,1... | collective-permute-start | bytes 393224 | tf_op jit(solution)/shard_map/ppermute | solution.py:207
  5.5 6.9 %collective-permute-start = (bf16[16,16,256]{2,1,0:T(8,128)(2,1)S(1)}, bf16[16,16,256]{2,1,0:T(8,128)(2,1)S(1)}, u32[]{:S(2)}, u32[]{:S(2)}) collective-permute-start(bf16[16,16,256]{2,1,0:T(8,128)(2,1)S(1)} %bitcast.52), channel_id=1, source_target_pairs={{0,1},{1,2},{2,3},{3,4},{4,5},{5,6},{6,7},{7,8},{8,9},{9,10},{10,1... | collective-permute-start | bytes 393224 | tf_op jit(solution)/shard_map/ppermute | solution.py:207
  13.3 16.3 %collective-permute-start.3 = (bf16[13,48,256]{2,1,0:T(8,128)(2,1)}, bf16[13,48,256]{2,1,0:T(8,128)(2,1)S(1)}, u32[]{:S(2)}, u32[]{:S(2)}) collective-permute-start(bf16[13,48,256]{2,1,0:T(8,128)(2,1)} %get-tuple-element.6), channel_id=1, source_target_pairs={{32,0},{64,32},{96,64},{128,96},{160,128},{192,160},{224,192},{256... | collective-permute-start | bytes 958472 | tf_op jit(solution)/shard_map/ppermute | solution.py:207
  22.2 7.4 %collective-permute-start.2 = (bf16[13,48,256]{2,1,0:T(8,128)(2,1)}, bf16[13,48,256]{2,1,0:T(8,128)(2,1)S(1)}, u32[]{:S(2)}, u32[]{:S(2)}) collective-permute-start(bf16[13,48,256]{2,1,0:T(8,128)(2,1)} %get-tuple-element.7), channel_id=1, source_target_pairs={{0,32},{32,64},{64,96},{96,128},{128,160},{160,192},{192,224},{224... | collective-permute-start | bytes 958472 | tf_op jit(solution)/shard_map/ppermute | solution.py:207
  24.2 5.4 %copy-start.1 = (bf16[16,16,256]{2,1,0:T(8,128)(2,1)S(1)}, bf16[16,16,256]{2,1,0:T(8,128)(2,1)}, u32[]{:S(2)}) copy-start(bf16[16,16,256]{2,1,0:T(8,128)(2,1)} %own.1) | copy-start | bytes 393220
  24.2 5.4 %copy-start.2 = (bf16[32,144]{1,0:T(8,128)(2,1)S(1)}, bf16[32,144]{1,0:T(8,128)(2,1)}, u32[]{:S(2)}) copy-start(bf16[32,144]{1,0:T(8,128)(2,1)} %constant.31.clone.inv_mat) | copy-start | bytes 27652
  24.2 5.4 %copy-start.3 = (bf16[48,96]{1,0:T(8,128)(2,1)S(1)}, bf16[48,96]{1,0:T(8,128)(2,1)}, u32[]{:S(2)}) copy-start(bf16[48,96]{1,0:T(8,128)(2,1)} %constant.29.clone.patch_mat) | copy-start | bytes 27652
  24.2 5.4 %copy-start.5 = (bf16[48,32]{1,0:T(8,128)(2,1)S(1)}, bf16[48,32]{1,0:T(8,128)(2,1)}, u32[]{:S(2)}) copy-start(bf16[48,32]{1,0:T(8,128)(2,1)} %constant.30.clone.tile_mat) | copy-start | bytes 9220
  67.4 38.8 %copy-start.8 = (bf16[27,27,256]{2,1,0:T(8,128)(2,1)S(1)}, bf16[27,27,256]{2,1,0:T(8,128)(2,1)}, u32[]{:S(2)}) copy-start(bf16[27,27,256]{2,1,0:T(8,128)(2,1)} %param.17) | copy-start | bytes 1119748
  101.6 4.7 %copy-start.4 = (bf16[48,64]{1,0:T(8,128)(2,1)S(1)}, bf16[48,64]{1,0:T(8,128)(2,1)}, u32[]{:S(2)}) copy-start(bf16[48,64]{1,0:T(8,128)(2,1)} %constant.32.clone.taps_mat) | copy-start | bytes 18436
  101.6 4.7 %copy-start.6 = (bf16[16,144]{1,0:T(8,128)(2,1)S(1)}, bf16[16,144]{1,0:T(8,128)(2,1)}, u32[]{:S(2)}) copy-start(bf16[16,144]{1,0:T(8,128)(2,1)} %constant.33.clone.inv_mat) | copy-start | bytes 13828
  102.6 13.8 %all-to-all-start.5 = ((bf16[16,176,128]{2,1,0:T(8,128)(2,1)}), bf16[16,176,128]{2,1,0:T(8,128)(2,1)S(1)}, u32[]{:S(2)}, u32[]{:S(2)}) async-start(bf16[16,176,128]{2,1,0:T(8,128)(2,1)} %broadcast_in_dim.22), calls=%async_computation.5 | async-start | bytes 1441792 | tf_op jit(solution)/shard_map/all_to_all | solution.py:247

commit v6 on v5

--- a/solution.py
+++ b/solution.py
@@ -71,10 +71,11 @@
     lax.fori_loop(0, pixels_ref.shape[0] // unroll, some, 0)
 
 
-def transform_patch(matrix_ref, low, wide, high, out_ref):
-    transform(matrix_ref, low, out_ref, 0, low.shape[0])
+def transform_patch(matrix_ref, core, far, wide, near, out_ref):
+    below = RADIUS + TILE
+    transform(matrix_ref, far, out_ref, core[0] * below, far.shape[0])
     transform(matrix_ref, wide, out_ref, RADIUS, 8)
-    transform(matrix_ref, high, out_ref, RADIUS + TILE, high.shape[0])
+    transform(matrix_ref, near, out_ref, (1 - core[0]) * below, near.shape[0])
 
 
 def back(matrix_ref, spectrum_ref, row):
@@ -99,9 +100,9 @@
     lax.fori_loop(0, 2, lane_step, 0)
 
 
-def taps_kernel(low, centre, high, own, patch_mat, tile_mat, inv_mat, out_ref, wide, tile, sums):
+def taps_kernel(core, far, centre, near, own, patch_mat, tile_mat, inv_mat, out_ref, wide, tile, sums):
     transform(tile_mat, own, tile, 0, 8)
-    transform_patch(patch_mat, low, centre, high, wide)
+    transform_patch(patch_mat, core, far, centre, near, wide)
     block = 9
 
     def work(re, im):
@@ -131,9 +132,9 @@
     out_ref[KS * KS :, :] = jnp.zeros((out_ref.shape[0] - KS * KS, out_ref.shape[1]), jnp.float32)
 
 
-def conv_kernel(low, centre, high, taps, grad, patch_mat, taps_mat, inv_mat, out_ref, wide, filt, sums):
+def conv_kernel(core, far, centre, near, taps, grad, patch_mat, taps_mat, inv_mat, out_ref, wide, filt, sums):
     transform(taps_mat, taps, filt, 0, 9)
-    transform_patch(patch_mat, low, centre, high, wide)
+    transform_patch(patch_mat, core, far, centre, near, wide)
     block = 8
 
     def work(re, im):
@@ -163,11 +164,12 @@
 
 
 def spectral_call(kernel, out_shape, second_rows, sum_rows, args):
+    vmem = pl.BlockSpec(memory_space=pltpu.VMEM)
     return pl.pallas_call(
         kernel,
         out_shape=out_shape,
-        in_specs=[pl.BlockSpec(memory_space=pltpu.VMEM)] * len(args),
-        out_specs=pl.BlockSpec(memory_space=pltpu.VMEM),
+        in_specs=[pl.BlockSpec(memory_space=pltpu.SMEM)] + [vmem] * (len(args) - 1),
+        out_specs=vmem,
         scratch_shapes=[
             pltpu.VMEM((PATCH, 2 * CELLS, 8, LANES), jnp.float32),
             pltpu.VMEM((second_rows, 2 * CELLS, 8, LANES), jnp.float32),
@@ -207,12 +209,22 @@
     return lax.ppermute(block, axes, pairs)
 
 
+def swapped(block, axes, first):
+    count = lax.axis_size(axes)
+    pairs = []
+    for i in range(first, count - 1, 2):
+        pairs += [(i, i + 1), (i + 1, i)]
+    return lax.ppermute(block, axes, pairs)
+
+
 def halo(block):
     left, right = shifted(block, COL, 1), shifted(block, COL, -1)
     wide = jnp.concatenate([left, block, right], axis=1)
-    low = shifted(wide[-RADIUS:], ROW, 1)
-    high = shifted(wide[:RADIUS], ROW, -1)
-    return (low, wide, high)
+    core = lax.axis_index("core")
+    spare = block.shape[0] - RADIUS
+    far = swapped(lax.dynamic_slice_in_dim(wide, core * spare, RADIUS, 0), ROW, 1)
+    near = swapped(lax.dynamic_slice_in_dim(wide, (1 - core) * spare, RADIUS, 0), ROW, 0)
+    return (core.reshape(1), far, wide, near)
 
 
 def gelu_parts(values):
@@ -254,9 +266,13 @@
         halves.append(scatter_sum(flat, "core").astype(jnp.bfloat16))
     part = scatter_sum(jnp.concatenate(halves, axis=0), PLANE)
     total = (scatter_sum(part, "z") * scale).astype(jnp.bfloat16)
-    both = gathered(gathered(gathered(total, "z"), PLANE), "core").reshape(2, -1, LANES)
+    run = gathered(total, "z")
+    own = gathered(run, PLANE)
+    other = swapped(own, ROW, 0)
+    first = lax.axis_index("core") == 0
+    pair = (jnp.where(first, own, other), jnp.where(first, other, own))
     split = halves[0].shape[0]
-    return both[:, :split].reshape(-1, LANES), both[:, split:].reshape(-1, LANES)
+    return [jnp.concatenate([half[rows] for half in pair], axis=0) for rows in (slice(0, split), slice(split, None))]
 
 
 def block_backward(inputs, stored, upstream, weight_in, weight_out, kernel):

time: 128 us -> 131 us (1.023)
  starting transfers between devices: 20.9 us -> 23.7 us
  waiting for transfers between devices: 4.75 us -> 2 us
    ppermute x0 -> x3, starting transfers between devices: none -> 17.4 us  [swapped(): return lax.ppermute(block, axes, pairs)]
    ppermute x4 -> x2, starting transfers between devices: 17.2 us -> 6.29 us  [shifted(): return lax.ppermute(block, axes, pairs)]
    all_to_all x1 -> x0, waiting for transfers between devices: 4.21 us -> none  [gathered(): lax.all_to_all(copies, axes, 0, 0).reshape(count * block.shape[0], LANES)]
    all_to_all x2, blocking collectives: 25.9 us -> 30.1 us  [gathered(): lax.all_to_all(copies, axes, 0, 0).reshape(count * block.shape[0], LANES)]
    all_to_all x1 -> x0, starting transfers between devices: 3.69 us -> none  [gathered(): lax.all_to_all(copies, axes, 0, 0).reshape(count * block.shape[0], LANES)]
    all_to_all x4, blocking collectives: 54.9 us -> 52 us  [scatter_sum(): arrived = lax.all_to_all(parts, axes, 0, 0)]
    ppermute x0 -> x3, waiting for transfers between devices: none -> 1.77 us  [swapped(): return lax.ppermute(block, axes, pairs)]
  transfers between devices with their start and end apart: 5 -> 5, of which waited for: 2 -> 2; matrix products, arithmetic and copies ran while one was open for 2% -> 2% of each run, Pallas kernels for 5% -> 4%
where the time goes in v6:
time: 131 us; the launch traced here: 130 us
  blocking collectives  82.1 us (63%)
  starting transfers between devices  23.7 us (18%)
  Pallas kernels  10.5 us (8%)
  local copies, waits for them, and re-layouts  6.47 us (5%)
  matrix products  3.26 us (2%)
  waiting for transfers between devices  2 us (2%)
    all_to_all x4, blocking collectives, scatter_sum(): arrived = lax.all_to_all(parts, axes, 0, 0)  52 us
    all_to_all x2, blocking collectives, gathered(): lax.all_to_all(copies, axes, 0, 0).reshape(count * block.shape[0], LANES)  30.1 us
    ppermute x3, starting transfers between devices, swapped(): return lax.ppermute(block, axes, pairs)  17.4 us
    pallas_call x2, Pallas kernels, spectral_call(): pl.pallas_call(kernel, out_shape=out_shape, in_specs=[pl.BlockSpec(memory...  10.5 us
    ppermute x2, starting transfers between devices, shifted(): return lax.ppermute(block, axes, pairs)  6.29 us
  transfers between devices with their start and end apart: 5, of which 2 were waited for; matrix products, arithmetic and copies ran while one was open for 2% of the time, Pallas kernels for 4%

profile of v6, /device:TPU:1, one launch (start us, length us, event | category | flops | bytes accessed | tf_op | source)
XLA Modules:
  0.0 130.1 jit_solution(12317829735787992150)
XLA Ops:
  0.6 0.0 copy-start
  0.6 0.0 copy-start.9
  0.7 0.0 copy-start.8
  0.7 1.0 copy-done
  1.7 1.2 fusion.16
  2.9 0.0 copy-done.9
  2.9 0.0 copy-done.8
  2.9 0.8 fusion
  3.7 0.3 fusion.2
  4.0 1.3 collective-permute-start.1
  5.3 5.0 %collective-permute-start = (bf16[16,16,256]{2,1,0:T(8,128)(2,1)S(1)}, bf16[16,16,256]{2,1,0:T(8,128)(2,1)S(1)}, u32[]{:S(2)}, u32[]{:S(2)}) collective-permute-start(bf16[16,16,256]{2,1,0:T(8,128)(2,1)S(1)} %bitcast.55), channel_id=1, source_target_pairs={{0,1},{1,2},{2,3},{3,4},{4,5},{5,6},{6,7},{7,8},{8,9},{9,10},{10,1... | collective-permute-start | bytes 393224 | tf_op jit(solution)/shard_map/ppermute | solution.py:209
  10.4 0.0 copy-start.7
  10.4 0.6 convolution_convert_fusion
  11.0 0.3 copy-done.7
  11.3 0.4 fusion.1
  11.6 0.2 copy.18
  11.8 0.1 copy.22
  11.9 0.1 copy.19
  12.0 0.0 collective-permute-done.1
  12.0 0.2 collective-permute-done
  12.3 0.9 constant_dynamic-slice_fusion
  13.2 8.9 %collective-permute-start.3 = (bf16[13,48,256]{2,1,0:T(8,128)(2,1)}, bf16[13,48,256]{2,1,0:T(8,128)(2,1)S(1)}, u32[]{:S(2)}, u32[]{:S(2)}) collective-permute-start(bf16[13,48,256]{2,1,0:T(8,128)(2,1)} %get-tuple-element.6), channel_id=1, source_target_pairs={{0,32},{32,0},{64,96},{96,64},{128,160},{160,128},{192,224},{224,1... | collective-permute-start | bytes 958472 | tf_op jit(solution)/shard_map/ppermute | solution.py:217
  22.1 1.9 %collective-permute-start.2 = (bf16[13,48,256]{2,1,0:T(8,128)(2,1)}, bf16[13,48,256]{2,1,0:T(8,128)(2,1)S(1)}, u32[]{:S(2)}, u32[]{:S(2)}) collective-permute-start(bf16[13,48,256]{2,1,0:T(8,128)(2,1)} %get-tuple-element.7), channel_id=1, source_target_pairs={{32,64},{64,32},{96,128},{128,96},{160,192},{192,160},{224,256},{2... | collective-permute-start | bytes 958472 | tf_op jit(solution)/shard_map/ppermute | solution.py:217
  24.0 0.1 pad_maximum_fusion
  24.1 4.2 %all_to_all.30 = bf16[2,2048,128]{2,1,0:T(8,128)(2,1)S(1)} all-to-all(bf16[2,2048,128]{2,1,0:T(8,128)(2,1)S(1)} %bitcast.58), channel_id=1, replica_groups=mesh['yh'=2,'x'=4,'core'=2,'yl'=2,'z'=16] {'core'}, dimensions={0} | all-to-all | bytes 2097152 | tf_op jit(solution)/shard_map/all_to_all | solution.py:252
  28.3 0.0 copy-start.1
  28.3 0.0 copy-start.2
  28.3 0.0 copy-start.3
  28.3 0.0 copy-start.5
  28.3 0.5 reduce_sum.42
  28.8 0.0 collective-permute-done.3.near
  28.8 1.8 %collective-permute-done.2.far = bf16[13,48,256]{2,1,0:T(8,128)(2,1)S(1)} collective-permute-done((bf16[13,48,256]{2,1,0:T(8,128)(2,1)}, bf16[13,48,256]{2,1,0:T(8,128)(2,1)S(1)}, u32[]{:S(2)}, u32[]{:S(2)}) %collective-permute-start.2) | collective-permute-done | bytes 319520 | tf_op jit(solution)/shard_map/ppermute | solution.py:217
  30.6 0.0 copy-done.1
  30.6 0.0 copy-done.2
  30.6 0.0 copy-done.3
  30.6 0.0 copy-done.5
  30.6 4.6 %shard_map.148 = f32[768,256]{1,0:T(8,128)S(1)} custom-call(s32[1]{0:T(128)} %bitcast.core, bf16[13,48,256]{2,1,0:T(8,128)(2,1)S(1)} %collective-permute-done.2.far, bf16[16,48,256]{2,1,0:T(8,128)(2,1)S(1)} %pad_maximum_fusion.2.centre, bf16[13,48,256]{2,1,0:T(8,128)(2,1)S(1)} %collective-permute-done.3.near, bf16[16,16,256]{2,1,0:T(8,128)(2,1)S(1)} %copy-done.1, ...), custom_call_target="tpu_custom_call" | custom-call | flops 4000000000 | bytes 8000000 | tf_op jit(solution)/shard_map/pallas_call | solution.py:168
  35.3 3.7 %all_to_all.31 = bf16[2,768,128]{2,1,0:T(8,128)(2,1)S(1)} all-to-all(bf16[2,768,128]{2,1,0:T(8,128)(2,1)S(1)} %bitcast.64), channel_id=1, replica_groups=mesh['yh'=2,'x'=4,'core'=2,'yl'=2,'z'=16] {'core'}, dimensions={0} | all-to-all | bytes 786432 | tf_op jit(solution)/shard_map/all_to_all | solution.py:252
  39.0 0.1 reduce_sum.43
  39.2 27.7 %all_to_all.32 = bf16[16,176,128]{2,1,0:T(8,128)(2,1)S(1)} all-to-all(bf16[16,176,128]{2,1,0:T(8,128)(2,1)S(1)} %bitcast.59), channel_id=1, replica_groups=mesh['yh'=2,'x'=4,'core'=2,'yl'=2,'z'=16] {'x','yh','yl'}, dimensions={0} | all-to-all | bytes 1441792 | tf_op jit(solution)/shard_map/all_to_all | solution.py:252
  66.9 0.1 convert_reduce_fusion
  67.0 16.3 %all_to_all.33 = f32[16,11,128]{2,1,0:T(8,128)S(1)} all-to-all(f32[16,11,128]{2,1,0:T(8,128)S(1)} %reshape.84), channel_id=1, replica_groups=mesh['yh'=2,'x'=4,'core'=2,'yl'=2,'z'=16] {'z'}, dimensions={0} | all-to-all | bytes 180224 | tf_op jit(solution)/shard_map/all_to_all | solution.py:252
  83.4 16.8 %all_to_all.34 = bf16[16,11,128]{2,1,0:T(8,128)(2,1)S(1)} all-to-all(bf16[16,11,128]{2,1,0:T(8,128)(2,1)S(1)} %broadcast_in_dim.6), channel_id=1, replica_groups=mesh['yh'=2,'x'=4,'core'=2,'yl'=2,'z'=16] {'z'}, dimensions={0} | all-to-all | bytes 90112 | tf_op jit(solution)/shard_map/all_to_all | solution.py:259
  100.2 0.1 broadcast_in_dim.15
  100.3 0.0 copy-start.4
  100.3 0.0 copy-start.6
  100.3 13.4 %all_to_all.35 = bf16[16,176,128]{2,1,0:T(8,128)(2,1)S(1)} all-to-all(bf16[16,176,128]{2,1,0:T(8,128)(2,1)S(1)} %broadcast_in_dim.15), channel_id=1, replica_groups=mesh['yh'=2,'x'=4,'core'=2,'yl'=2,'z'=16] {'x','yh','yl'}, dimensions={0} | all-to-all | bytes 1441792 | tf_op jit(solution)/shard_map/all_to_all | solution.py:259
  113.7 6.6 %collective-permute-start.4 = (bf16[2816,128]{1,0:T(8,128)(2,1)S(1)}, bf16[2816,128]{1,0:T(8,128)(2,1)S(1)}, u32[]{:S(2)}, u32[]{:S(2)}) collective-permute-start(bf16[2816,128]{1,0:T(8,128)(2,1)S(1)} %bitcast.60), channel_id=1, source_target_pairs={{0,32},{32,0},{64,96},{96,64},{128,160},{160,128},{192,224},{224,1... | collective-permute-start | bytes 2162696 | tf_op jit(solution)/shard_map/ppermute | solution.py:217
  120.3 1.1 pad.4.taps
  121.4 0.0 copy-done.4
  121.4 0.0 copy-done.6
  121.4 5.8 %shard_map.147 = bf16[16,16,256]{2,1,0:T(8,128)(2,1)} custom-call(s32[1]{0:T(128)} %bitcast.core, bf16[13,48,256]{2,1,0:T(8,128)(2,1)S(1)} %collective-permute-done.2.far, bf16[16,48,256]{2,1,0:T(8,128)(2,1)S(1)} %pad_maximum_fusion.2.centre, bf16[13,48,256]{2,1,0:T(8,128)(2,1)S(1)} %collective-permute-done.3.near, bf16[27,32,256]{2,1,0:T(8,128)(2,1)S(1)} %pad.4.taps, ...), custom_call_target="tpu_custom_call" | custom-call | flops 4000000000 | bytes 8000000 | tf_op jit(solution)/shard_map/pallas_call | solution.py:168
  127.3 0.0 collective-permute-done.4
  127.3 0.1 broadcast_select_fusion
  127.4 0.8 slice.21
  128.3 0.8 slice.20
  129.2 0.9 reshape.92
  (12 shorter events, 0.3 us)
Async XLA Ops:
  0.6 1.0 copy-start
  0.6 2.2 %copy-start.9 = (bf16[1024,256]{1,0:T(8,128)(2,1)S(1)}, bf16[1024,256]{1,0:T(8,128)(2,1)}, u32[]{:S(2)}) copy-start(bf16[1024,256]{1,0:T(8,128)(2,1)} %param.16) | copy-start | bytes 1572868
  0.7 2.2 %copy-start.8 = (bf16[16,16,256]{2,1,0:T(8,128)(2,1)S(1)}, bf16[16,16,256]{2,1,0:T(8,128)(2,1)}, u32[]{:S(2)}) copy-start(bf16[16,16,256]{2,1,0:T(8,128)(2,1)} %param.14) | copy-start | bytes 393220
  4.0 8.0 %collective-permute-start.1 = (bf16[16,16,256]{2,1,0:T(8,128)(2,1)S(1)}, bf16[16,16,256]{2,1,0:T(8,128)(2,1)S(1)}, u32[]{:S(2)}, u32[]{:S(2)}) collective-permute-start(bf16[16,16,256]{2,1,0:T(8,128)(2,1)S(1)} %bitcast.54), channel_id=1, source_target_pairs={{1,0},{2,1},{3,2},{4,3},{5,4},{6,5},{7,6},{8,7},{9,8},{10,9},{11,1... | collective-permute-start | bytes 393224 | tf_op jit(solution)/shard_map/ppermute | solution.py:209
  5.3 6.9 %collective-permute-start = (bf16[16,16,256]{2,1,0:T(8,128)(2,1)S(1)}, bf16[16,16,256]{2,1,0:T(8,128)(2,1)S(1)}, u32[]{:S(2)}, u32[]{:S(2)}) collective-permute-start(bf16[16,16,256]{2,1,0:T(8,128)(2,1)S(1)} %bitcast.55), channel_id=1, source_target_pairs={{0,1},{1,2},{2,3},{3,4},{4,5},{5,6},{6,7},{7,8},{8,9},{9,10},{10,1... | collective-permute-start | bytes 393224 | tf_op jit(solution)/shard_map/ppermute | solution.py:209
  10.4 0.9 copy-start.7
  13.2 15.6 %collective-permute-start.3 = (bf16[13,48,256]{2,1,0:T(8,128)(2,1)}, bf16[13,48,256]{2,1,0:T(8,128)(2,1)S(1)}, u32[]{:S(2)}, u32[]{:S(2)}) collective-permute-start(bf16[13,48,256]{2,1,0:T(8,128)(2,1)} %get-tuple-element.6), channel_id=1, source_target_pairs={{0,32},{32,0},{64,96},{96,64},{128,160},{160,128},{192,224},{224,1... | collective-permute-start | bytes 958472 | tf_op jit(solution)/shard_map/ppermute | solution.py:217
  22.1 8.5 %collective-permute-start.2 = (bf16[13,48,256]{2,1,0:T(8,128)(2,1)}, bf16[13,48,256]{2,1,0:T(8,128)(2,1)S(1)}, u32[]{:S(2)}, u32[]{:S(2)}) collective-permute-start(bf16[13,48,256]{2,1,0:T(8,128)(2,1)} %get-tuple-element.7), channel_id=1, source_target_pairs={{32,64},{64,32},{96,128},{128,96},{160,192},{192,160},{224,256},{2... | collective-permute-start | bytes 958472 | tf_op jit(solution)/shard_map/ppermute | solution.py:217
  28.3 2.3 %copy-start.1 = (bf16[16,16,256]{2,1,0:T(8,128)(2,1)S(1)}, bf16[16,16,256]{2,1,0:T(8,128)(2,1)}, u32[]{:S(2)}) copy-start(bf16[16,16,256]{2,1,0:T(8,128)(2,1)} %own.1) | copy-start | bytes 393220
  28.3 2.3 %copy-start.2 = (bf16[32,144]{1,0:T(8,128)(2,1)S(1)}, bf16[32,144]{1,0:T(8,128)(2,1)}, u32[]{:S(2)}) copy-start(bf16[32,144]{1,0:T(8,128)(2,1)} %constant.44.clone.inv_mat) | copy-start | bytes 27652
  28.3 2.3 %copy-start.3 = (bf16[48,96]{1,0:T(8,128)(2,1)S(1)}, bf16[48,96]{1,0:T(8,128)(2,1)}, u32[]{:S(2)}) copy-start(bf16[48,96]{1,0:T(8,128)(2,1)} %constant.42.clone.patch_mat) | copy-start | bytes 27652
  28.3 2.3 %copy-start.5 = (bf16[48,32]{1,0:T(8,128)(2,1)S(1)}, bf16[48,32]{1,0:T(8,128)(2,1)}, u32[]{:S(2)}) copy-start(bf16[48,32]{1,0:T(8,128)(2,1)} %constant.43.clone.tile_mat) | copy-start | bytes 9220
  100.3 21.1 %copy-start.4 = (bf16[48,64]{1,0:T(8,128)(2,1)S(1)}, bf16[48,64]{1,0:T(8,128)(2,1)}, u32[]{:S(2)}) copy-start(bf16[48,64]{1,0:T(8,128)(2,1)} %constant.45.clone.taps_mat) | copy-start | bytes 18436
  100.3 21.1 %copy-start.6 = (bf16[16,144]{1,0:T(8,128)(2,1)S(1)}, bf16[16,144]{1,0:T(8,128)(2,1)}, u32[]{:S(2)}) copy-start(bf16[16,144]{1,0:T(8,128)(2,1)} %constant.46.clone.inv_mat) | copy-start | bytes 13828
  113.7 13.6 %collective-permute-start.4 = (bf16[2816,128]{1,0:T(8,128)(2,1)S(1)}, bf16[2816,128]{1,0:T(8,128)(2,1)S(1)}, u32[]{:S(2)}, u32[]{:S(2)}) collective-permute-start(bf16[2816,128]{1,0:T(8,128)(2,1)S(1)} %bitcast.60), channel_id=1, source_target_pairs={{0,32},{32,0},{64,96},{96,64},{128,160},{160,128},{192,224},{224,1... | collective-permute-start | bytes 2162696 | tf_op jit(solution)/shard_map/ppermute | solution.py:217
